TPU v7x, 512 devices: a whole 4x4x16 slice. The times are simulated.
512 devices in a mesh: dp: 4 (over x), ctx: 32 (over z, core), ch: 4 (over y).
Axes of the slice: x: 4, y: 4, z: 16, core: 2. Of those that a mesh axis runs over, the one named last changes fastest.
Arguments:
- gate_input: bfloat16 [4, 4096, 4096], P('dp', 'ctx', 'ch'), may hold values from -6 to 6
- conv_input: bfloat16 [4, 4096, 4096], P('dp', 'ctx', 'ch'), may hold values from -6 to 6
- grad_output: bfloat16 [4, 4096, 4096], P('dp', 'ctx', 'ch'), may hold values from -6 to 6
- kernel: bfloat16 [128, 640], P('ch'), may hold values from -0.25 to 0.25
Outputs:
- output: bfloat16 [4, 4096, 4096], P('dp', 'ctx', 'ch')
- grad_gate: bfloat16 [4, 4096, 4096], P('dp', 'ctx', 'ch')
- grad_conv: bfloat16 [4, 4096, 4096], P('dp', 'ctx', 'ch')
- grad_kernel: float32 [128, 640], P('ch', ('dp', 'ctx'))
All inputs are finite; a program needn't handle non-finite values.
Results may differ from a plain program's by a relative error of at most 0.0049.
Values may be sent and summed in bfloat16 or wider, within the bound.
No kernel may reach another device: no remote copies, remote signals or barrier semaphores. Data moves between devices by JAX's collectives and lax.ppermute only.
A program may use at most 64 MiB of HBM per device.

v0:
```python
import math

import jax
import jax.numpy as jnp
from jax import lax
from jax.sharding import PartitionSpec as P


def passed_along(x, axis, by):
    length = lax.axis_size(axis)
    pairs = [(i, i + by) for i in range(length) if 0 <= i + by < length]
    return lax.ppermute(x, axis, pairs)


def toeplitz(padded_kernel, offset, tok_rows):
    groups = padded_kernel.shape[0]
    segment = lax.dynamic_slice_in_dim(padded_kernel, offset * tok_rows + 1, 2 * tok_rows, 1)
    reverse = segment[:, ::-1]
    rolled = jnp.concatenate([reverse[:, tok_rows:], reverse[:, :tok_rows]], axis=1)
    tiled = jnp.tile(rolled, (1, tok_rows))[:, : tok_rows * (2 * tok_rows - 1)]
    return tiled.reshape(groups, tok_rows, 2 * tok_rows - 1)[:, :, :tok_rows]


def diagonal_sums(matrix):
    groups = matrix.shape[0]
    extent = matrix.shape[1]
    flipped = matrix[:, :, ::-1]
    padded = jnp.pad(flipped, ((0, 0), (0, 0), (0, extent)))
    flattened = padded.reshape(groups, 2 * extent * extent)[:, : extent * (2 * extent - 1)]
    totals = jnp.sum(flattened.reshape(groups, extent, 2 * extent - 1), axis=1, dtype=jnp.float32)
    return jnp.pad(totals, ((0, 0), (0, 1)))


def shards(gate_input, conv_input, grad_output, kernel):
    tok_rows = gate_input.shape[1]
    channels = gate_input.shape[2]
    groups = kernel.shape[0]
    group_size = channels // groups
    lag_count = kernel.shape[1]
    lag_blocks = lag_count // tok_rows
    padded_kernel = jnp.pad(kernel, ((0, 0), (tok_rows, 2 * tok_rows)))
    blocks = lax.axis_size("ctx")
    own_block = lax.axis_index("ctx")
    gate_rows = gate_input[0]
    value_rows = conv_input[0]
    grad_rows = grad_output[0]
    grad_mixed = (gate_rows.astype(jnp.float32) * grad_rows.astype(jnp.float32)).astype(
        jnp.bfloat16
    )

    def forward_add(running, matrix, block):
        shaped = block.reshape(tok_rows, groups, group_size)
        return running + jnp.einsum(
            "gab,bgc->agc", matrix, shaped, preferred_element_type=jnp.float32
        ).reshape(tok_rows, channels)

    def backward_add(running, matrix, block):
        shaped = block.reshape(tok_rows, groups, group_size)
        return running + jnp.einsum(
            "gab,agc->bgc", matrix, shaped, preferred_element_type=jnp.float32
        ).reshape(tok_rows, channels)

    def window_add(buffer, grad_block, value_block, offset):
        left_side = grad_block.reshape(tok_rows, groups, group_size)
        right_side = value_block.reshape(tok_rows, groups, group_size)
        paired = jnp.einsum(
            "agc,bgc->gab", left_side, right_side, preferred_element_type=jnp.float32
        ).astype(jnp.bfloat16)
        window = diagonal_sums(paired)
        first_col = offset * tok_rows
        current = lax.dynamic_slice_in_dim(buffer, first_col, 2 * tok_rows, 1)
        return lax.dynamic_update_slice_in_dim(buffer, current + window, first_col, 1)

    def visit_block(carried, value_block, grad_block, offset, has_value, has_grad):
        convolved, grad_vals, buffer = carried
        bounded = jnp.minimum(offset, lag_blocks)
        matrix = toeplitz(padded_kernel, bounded, tok_rows)
        convolved = lax.cond(
            has_value, lambda: forward_add(convolved, matrix, value_block), lambda: convolved
        )
        grad_vals = lax.cond(
            has_grad, lambda: backward_add(grad_vals, matrix, grad_block), lambda: grad_vals
        )
        buffer = lax.cond(
            has_value, lambda: window_add(buffer, grad_mixed, value_block, bounded), lambda: buffer
        )
        return (convolved, grad_vals, buffer)

    initial = (
        jnp.zeros((tok_rows, channels), jnp.float32),
        jnp.zeros((tok_rows, channels), jnp.float32),
        jnp.zeros((groups, lag_count + 2 * tok_rows), jnp.float32),
    )
    zero_offset = jnp.zeros((), jnp.int32)
    carried = visit_block(
        initial, value_rows, grad_mixed, zero_offset, jnp.array(True), jnp.array(True)
    )

    def advance(offset, packed):
        carried_now, value_now, grad_now = packed
        value_now = passed_along(value_now, "ctx", 1)
        grad_now = passed_along(grad_now, "ctx", -1)
        carried_now = visit_block(
            carried_now,
            value_now,
            grad_now,
            offset,
            own_block - offset >= 0,
            own_block + offset <= blocks - 1,
        )
        return (carried_now, value_now, grad_now)

    carried, value_last, grad_last = lax.fori_loop(
        1, lag_blocks + 1, advance, (carried, value_rows, grad_mixed)
    )
    convolved, grad_vals, buffer = carried
    output = (gate_rows.astype(jnp.float32) * convolved).astype(jnp.bfloat16)[None]
    grad_gate = (grad_rows.astype(jnp.float32) * convolved).astype(jnp.bfloat16)[None]
    grad_conv = grad_vals.astype(jnp.bfloat16)[None]
    partial_value = buffer[:, tok_rows - 1 : tok_rows - 1 + lag_count]
    summed = lax.psum_scatter(partial_value, ("dp", "ctx"), scatter_dimension=1, tiled=True)
    grad_kernel = summed / math.sqrt(lax.axis_size("dp") * tok_rows * blocks)
    return (output, grad_gate, grad_conv, grad_kernel)


def solution(mesh):
    return jax.shard_map(
        shards,
        mesh=mesh,
        in_specs=(P("dp", "ctx", "ch"), P("dp", "ctx", "ch"), P("dp", "ctx", "ch"), P("ch", None)),
        out_specs=(
            P("dp", "ctx", "ch"),
            P("dp", "ctx", "ch"),
            P("dp", "ctx", "ch"),
            P("ch", ("dp", "ctx")),
        ),
        check_vma=False,
    )
```

profile of v0, /device:TPU:24, one launch (start us, length us, event | category | flops | bytes accessed | tf_op | source)
XLA Modules:
  0.0 637.1 jit_solution(2158315386110350615)
XLA Ops:
  10.9 7.8 %reshape.77 = bf16[32,128,255]{2,1,0:T(8,128)(2,1)} reshape(bf16[32,32640]{1,0:T(8,128)(2,1)S(1)} %slice.87) | data formatting | bytes 4177920 | tf_op jit(solution)/shard_map/reshape | solution.py:21
  19.1 2.0 fusion.2
  23.0 11.0 %rev.10 = bf16[32,128,128]{2,1,0:T(8,128)(2,1)} reverse(bf16[32,128,128]{2,1,0:T(8,128)(2,1)S(1)} %convolution_convert_fusion.1), dimensions={2} | reverse | bytes 2097152 | tf_op jit(solution)/shard_map/cond/branch_1_fun/rev | solution.py:27
  37.5 2.2 slice_convert_fusion.1
  39.7 9.4 %reshape.83 = f32[32,128,255]{2,1,0:T(8,128)} reshape(f32[32,32640]{1,0:T(8,128)} %slice_convert_fusion.1) | data formatting | bytes 8355840 | tf_op jit(solution)/shard_map/cond/branch_1_fun/convert_element_type | solution.py:30
  49.1 2.6 reduce_sum.18
  52.4 170.7 %while.32 = (s32[]{:T(128)}, f32[128,1024]{0,1:T(8,128)S(1)}, f32[128,1024]{0,1:T(8,128)}, f32[32,896]{1,0:T(8,128)S(1)}, bf16[128,1024]{0,1:T(8,128)(2,1)S(1)},...) while((s32[]{:T(128)}, f32[128,1024]{0,1:T(8,128)S(1)}, ...), condition=%wide.region_9.10_spmd, body=%wide.region_1.9_spmd.sunk | while | flops 103571504 | bytes 64102940 | solution.py:113
  52.4 1.7 collective-permute-start
  58.1 7.8 %reshape.87 = bf16[32,128,255]{2,1,0:T(8,128)(2,1)} reshape(bf16[32,32640]{1,0:T(8,128)(2,1)S(1)} %slice.105) | data formatting | bytes 4177920 | tf_op jit(solution)/shard_map/while/body/eval_jaxpr/reshape | solution.py:21
  68.0 3.3 conditional.7
  69.5 1.9 bitcast_add_fusion.1
  71.4 1.7 copy.65
  73.1 26.4 %collective-permute-start = (bf16[128,1024]{0,1:T(8,128)(2,1)S(1)}, bf16[128,1024]{0,1:T(8,128)(2,1)S(1)}, u32[]{:S(2)}, u32[]{:S(2)}) collective-permute-start(bf16[128,1024]{0,1:T(8,128)(2,1)S(1)} %get-tuple-element.412), channel_id=1, source_target_pairs={{0,4},{4,8},{8,12},{12,16},{16,20},{20,24},{24,28},{28,32},{32,36}... | collective-permute-start | bytes 786440 | tf_op jit(solution)/shard_map/while/body/eval_jaxpr/ppermute | solution.py:12
  103.3 7.8 %reshape.87 = bf16[32,128,255]{2,1,0:T(8,128)(2,1)} reshape(bf16[32,32640]{1,0:T(8,128)(2,1)S(1)} %slice.105) | data formatting | bytes 4177920 | tf_op jit(solution)/shard_map/while/body/eval_jaxpr/reshape | solution.py:21
  113.3 3.3 conditional.7
  114.7 1.9 bitcast_add_fusion.1
  116.6 1.7 copy.65
  118.3 4.3 collective-permute-start
  126.5 7.8 %reshape.87 = bf16[32,128,255]{2,1,0:T(8,128)(2,1)} reshape(bf16[32,32640]{1,0:T(8,128)(2,1)S(1)} %slice.105) | data formatting | bytes 4177920 | tf_op jit(solution)/shard_map/while/body/eval_jaxpr/reshape | solution.py:21
  136.4 12.8 %collective-permute-done.1 = bf16[128,1024]{0,1:T(8,128)(2,1)} collective-permute-done((bf16[128,1024]{0,1:T(8,128)(2,1)}, bf16[128,1024]{0,1:T(8,128)(2,1)}, u32[]{:S(2)}, u32[]{:S(2)}) %collective-permute-start.1) | collective-permute-done | bytes 262176 | tf_op jit(solution)/shard_map/while/body/eval_jaxpr/ppermute | solution.py:12
  149.2 3.3 conditional.7
  150.6 1.9 bitcast_add_fusion.1
  154.3 13.1 %collective-permute-start = (bf16[128,1024]{0,1:T(8,128)(2,1)S(1)}, bf16[128,1024]{0,1:T(8,128)(2,1)S(1)}, u32[]{:S(2)}, u32[]{:S(2)}) collective-permute-start(bf16[128,1024]{0,1:T(8,128)(2,1)S(1)} %get-tuple-element.412), channel_id=1, source_target_pairs={{0,4},{4,8},{8,12},{12,16},{16,20},{20,24},{24,28},{28,32},{32,36}... | collective-permute-start | bytes 786440 | tf_op jit(solution)/shard_map/while/body/eval_jaxpr/ppermute | solution.py:12
  171.3 7.8 %reshape.87 = bf16[32,128,255]{2,1,0:T(8,128)(2,1)} reshape(bf16[32,32640]{1,0:T(8,128)(2,1)S(1)} %slice.105) | data formatting | bytes 4177920 | tf_op jit(solution)/shard_map/while/body/eval_jaxpr/reshape | solution.py:21
  181.2 3.3 conditional.7
  182.7 1.9 bitcast_add_fusion.1
  186.3 18.0 %collective-permute-start = (bf16[128,1024]{0,1:T(8,128)(2,1)S(1)}, bf16[128,1024]{0,1:T(8,128)(2,1)S(1)}, u32[]{:S(2)}, u32[]{:S(2)}) collective-permute-start(bf16[128,1024]{0,1:T(8,128)(2,1)S(1)} %get-tuple-element.412), channel_id=1, source_target_pairs={{0,4},{4,8},{8,12},{12,16},{16,20},{20,24},{24,28},{28,32},{32,36}... | collective-permute-start | bytes 786440 | tf_op jit(solution)/shard_map/while/body/eval_jaxpr/ppermute | solution.py:12
  208.1 7.8 %reshape.87 = bf16[32,128,255]{2,1,0:T(8,128)(2,1)} reshape(bf16[32,32640]{1,0:T(8,128)(2,1)S(1)} %slice.105) | data formatting | bytes 4177920 | tf_op jit(solution)/shard_map/while/body/eval_jaxpr/reshape | solution.py:21
  218.1 3.3 conditional.7
  219.5 1.9 bitcast_add_fusion.1
  227.0 1.9 copy.31
  230.8 398.2 %all-reduce.9.cloned.1.call-done = f32[32,640]{0,1:T(8,128)} async-done(((f32[32,640]{0,1:T(8,128)}), f32[32,640]{0,1:T(8,128)}) %all-reduce.9.cloned.1.call-update) | async-done | bytes 81936
  (157 shorter events, 58.3 us)
Async XLA Ops:
  7.2 621.8 %all-reduce.9.cloned.1.call-start = ((), (), s32[]{:S(2)}) async-start(), calls=%async_computation | async-start | bytes 655360
  10.9 7.8 %copy-start.8 = (bf16[1,128,1024]{2,1,0:T(8,128)(2,1)S(1)}, bf16[1,128,1024]{2,1,0:T(8,128)(2,1)}, u32[]{:S(2)}) copy-start(bf16[1,128,1024]{2,1,0:T(8,128)(2,1)} %param.14) | copy-start | bytes 786436
  10.9 8.0 %copy-start.9 = (bf16[1,128,1024]{2,1,0:T(8,128)(2,1)S(1)}, bf16[1,128,1024]{2,1,0:T(8,128)(2,1)}, u32[]{:S(2)}) copy-start(bf16[1,128,1024]{2,1,0:T(8,128)(2,1)} %param.12) | copy-start | bytes 786436
  18.9 4.0 copy-start.6
  19.1 3.9 copy-start.7
  19.1 2.1 copy-start.5
  22.4 11.6 %copy-start.10 = (bf16[32,640]{1,0:T(8,128)(2,1)S(1)}, bf16[32,640]{1,0:T(8,128)(2,1)}, u32[]{:S(2)}) copy-start(bf16[32,640]{1,0:T(8,128)(2,1)} %param.15) | copy-start | bytes 122884
  52.4 14.8 %copy-start.2 = (bf16[128,1024]{0,1:T(8,128)(2,1)}, bf16[128,1024]{0,1:T(8,128)(2,1)S(1)}, u32[]{:S(2)}) copy-start(bf16[128,1024]{0,1:T(8,128)(2,1)S(1)} %get-tuple-element.432) | copy-start | bytes 786436 | tf_op jit(solution)/shard_map/while
  52.4 14.7 %collective-permute-start = (bf16[128,1024]{0,1:T(8,128)(2,1)S(1)}, bf16[128,1024]{0,1:T(8,128)(2,1)S(1)}, u32[]{:S(2)}, u32[]{:S(2)}) collective-permute-start(bf16[128,1024]{0,1:T(8,128)(2,1)S(1)} %get-tuple-element.412), channel_id=1, source_target_pairs={{0,4},{4,8},{8,12},{12,16},{16,20},{20,24},{24,28},{28,32},{32,36}... | collective-permute-start | bytes 786440 | tf_op jit(solution)/shard_map/while/body/eval_jaxpr/ppermute | solution.py:12
  54.2 13.8 %collective-permute-start.1 = (bf16[128,1024]{0,1:T(8,128)(2,1)}, bf16[128,1024]{0,1:T(8,128)(2,1)}, u32[]{:S(2)}, u32[]{:S(2)}) collective-permute-start(bf16[128,1024]{0,1:T(8,128)(2,1)} %get-tuple-element.413), channel_id=1, source_target_pairs={{4,0},{8,4},{12,8},{16,12},{20,16},{24,20},{28,24},{32,28},{36,32}... | collective-permute-start | bytes 786440 | tf_op jit(solution)/shard_map/while/body/eval_jaxpr/ppermute | solution.py:12
  68.0 5.0 copy-start.1
  68.0 5.0 copy-start.3
  73.1 39.4 %copy-start.2 = (bf16[128,1024]{0,1:T(8,128)(2,1)}, bf16[128,1024]{0,1:T(8,128)(2,1)S(1)}, u32[]{:S(2)}) copy-start(bf16[128,1024]{0,1:T(8,128)(2,1)S(1)} %get-tuple-element.432) | copy-start | bytes 786436 | tf_op jit(solution)/shard_map/while
  73.1 39.3 %collective-permute-start = (bf16[128,1024]{0,1:T(8,128)(2,1)S(1)}, bf16[128,1024]{0,1:T(8,128)(2,1)S(1)}, u32[]{:S(2)}, u32[]{:S(2)}) collective-permute-start(bf16[128,1024]{0,1:T(8,128)(2,1)S(1)} %get-tuple-element.412), channel_id=1, source_target_pairs={{0,4},{4,8},{8,12},{12,16},{16,20},{20,24},{24,28},{28,32},{32,36}... | collective-permute-start | bytes 786440 | tf_op jit(solution)/shard_map/while/body/eval_jaxpr/ppermute | solution.py:12
  99.4 13.8 %collective-permute-start.1 = (bf16[128,1024]{0,1:T(8,128)(2,1)}, bf16[128,1024]{0,1:T(8,128)(2,1)}, u32[]{:S(2)}, u32[]{:S(2)}) collective-permute-start(bf16[128,1024]{0,1:T(8,128)(2,1)} %get-tuple-element.413), channel_id=1, source_target_pairs={{4,0},{8,4},{12,8},{16,12},{20,16},{24,20},{28,24},{32,28},{36,32}... | collective-permute-start | bytes 786440 | tf_op jit(solution)/shard_map/while/body/eval_jaxpr/ppermute | solution.py:12
  113.3 5.0 copy-start.1
  113.3 5.0 copy-start.3
  118.3 17.3 %copy-start.2 = (bf16[128,1024]{0,1:T(8,128)(2,1)}, bf16[128,1024]{0,1:T(8,128)(2,1)S(1)}, u32[]{:S(2)}) copy-start(bf16[128,1024]{0,1:T(8,128)(2,1)S(1)} %get-tuple-element.432) | copy-start | bytes 786436 | tf_op jit(solution)/shard_map/while
  118.3 17.3 %collective-permute-start = (bf16[128,1024]{0,1:T(8,128)(2,1)S(1)}, bf16[128,1024]{0,1:T(8,128)(2,1)S(1)}, u32[]{:S(2)}, u32[]{:S(2)}) collective-permute-start(bf16[128,1024]{0,1:T(8,128)(2,1)S(1)} %get-tuple-element.412), channel_id=1, source_target_pairs={{0,4},{4,8},{8,12},{12,16},{16,20},{20,24},{24,28},{28,32},{32,36}... | collective-permute-start | bytes 786440 | tf_op jit(solution)/shard_map/while/body/eval_jaxpr/ppermute | solution.py:12
  122.6 26.6 %collective-permute-start.1 = (bf16[128,1024]{0,1:T(8,128)(2,1)}, bf16[128,1024]{0,1:T(8,128)(2,1)}, u32[]{:S(2)}, u32[]{:S(2)}) collective-permute-start(bf16[128,1024]{0,1:T(8,128)(2,1)} %get-tuple-element.413), channel_id=1, source_target_pairs={{4,0},{8,4},{12,8},{16,12},{20,16},{24,20},{28,24},{32,28},{36,32}... | collective-permute-start | bytes 786440 | tf_op jit(solution)/shard_map/while/body/eval_jaxpr/ppermute | solution.py:12
  149.2 5.0 copy-start.1
  149.2 5.0 copy-start.3
  154.3 26.1 %copy-start.2 = (bf16[128,1024]{0,1:T(8,128)(2,1)}, bf16[128,1024]{0,1:T(8,128)(2,1)S(1)}, u32[]{:S(2)}) copy-start(bf16[128,1024]{0,1:T(8,128)(2,1)S(1)} %get-tuple-element.432) | copy-start | bytes 786436 | tf_op jit(solution)/shard_map/while
  154.3 26.1 %collective-permute-start = (bf16[128,1024]{0,1:T(8,128)(2,1)S(1)}, bf16[128,1024]{0,1:T(8,128)(2,1)S(1)}, u32[]{:S(2)}, u32[]{:S(2)}) collective-permute-start(bf16[128,1024]{0,1:T(8,128)(2,1)S(1)} %get-tuple-element.412), channel_id=1, source_target_pairs={{0,4},{4,8},{8,12},{12,16},{16,20},{20,24},{24,28},{28,32},{32,36}... | collective-permute-start | bytes 786440 | tf_op jit(solution)/shard_map/while/body/eval_jaxpr/ppermute | solution.py:12
  167.4 13.8 %collective-permute-start.1 = (bf16[128,1024]{0,1:T(8,128)(2,1)}, bf16[128,1024]{0,1:T(8,128)(2,1)}, u32[]{:S(2)}, u32[]{:S(2)}) collective-permute-start(bf16[128,1024]{0,1:T(8,128)(2,1)} %get-tuple-element.413), channel_id=1, source_target_pairs={{4,0},{8,4},{12,8},{16,12},{20,16},{24,20},{28,24},{32,28},{36,32}... | collective-permute-start | bytes 786440 | tf_op jit(solution)/shard_map/while/body/eval_jaxpr/ppermute | solution.py:12
  181.2 5.0 copy-start.1
  181.2 5.0 copy-start.3
  186.3 31.0 %copy-start.2 = (bf16[128,1024]{0,1:T(8,128)(2,1)}, bf16[128,1024]{0,1:T(8,128)(2,1)S(1)}, u32[]{:S(2)}) copy-start(bf16[128,1024]{0,1:T(8,128)(2,1)S(1)} %get-tuple-element.432) | copy-start | bytes 786436 | tf_op jit(solution)/shard_map/while
  186.3 31.0 %collective-permute-start = (bf16[128,1024]{0,1:T(8,128)(2,1)S(1)}, bf16[128,1024]{0,1:T(8,128)(2,1)S(1)}, u32[]{:S(2)}, u32[]{:S(2)}) collective-permute-start(bf16[128,1024]{0,1:T(8,128)(2,1)S(1)} %get-tuple-element.412), channel_id=1, source_target_pairs={{0,4},{4,8},{8,12},{12,16},{16,20},{20,24},{24,28},{28,32},{32,36}... | collective-permute-start | bytes 786440 | tf_op jit(solution)/shard_map/while/body/eval_jaxpr/ppermute | solution.py:12
  204.3 13.8 %collective-permute-start.1 = (bf16[128,1024]{0,1:T(8,128)(2,1)}, bf16[128,1024]{0,1:T(8,128)(2,1)}, u32[]{:S(2)}, u32[]{:S(2)}) collective-permute-start(bf16[128,1024]{0,1:T(8,128)(2,1)} %get-tuple-element.413), channel_id=1, source_target_pairs={{4,0},{8,4},{12,8},{16,12},{20,16},{24,20},{28,24},{32,28},{36,32}... | collective-permute-start | bytes 786440 | tf_op jit(solution)/shard_map/while/body/eval_jaxpr/ppermute | solution.py:12
  218.1 5.0 copy-start.1
  218.1 5.0 copy-start.3
  (5 other events, 4.2 us)
Sparse Core Ops, SparseCore 0:
  224.2 404.6 all-reduce.8
where the time goes:
time: 639 us; the launch traced here: 637 us
  waiting for transfers between devices  411 us (64%)
  local copies, waits for them, and re-layouts  113 us (18%)
  starting transfers between devices  70 us (11%)
  other arithmetic  17.1 us (3%)
  between operations  14.9 us (2%)
  matrix products  10.7 us (2%)
    unnamed x2, waiting for transfers between devices  398 us
    ppermute x10, starting transfers between devices, passed_along(): return lax.ppermute(x, axis, pairs)  69.9 us
    reshape x6, local copies, waits for them, and re-layouts, toeplitz(): return tiled.reshape(groups, tok_rows, 2 * tok_rows - 1)[:, :, :tok_rows]  46.7 us
    while x55, local copies, waits for them, and re-layouts  18.6 us
    ppermute x10, waiting for transfers between devices, passed_along(): return lax.ppermute(x, axis, pairs)  12.8 us
  transfers between devices with their start and end apart: 11, of which 2 were waited for; matrix products, arithmetic and copies ran while one was open for 10% of the time, Pallas kernels for 0%

commit v1 on v0

v1 whole, which is shorter than its diff:
```python
import math

import jax
import jax.numpy as jnp
from jax import lax
from jax.experimental import pallas as pl
from jax.experimental.pallas import tpu as pltpu
from jax.sharding import PartitionSpec as P

LANES = 128


def passed_along(x, axis, by):
    length = lax.axis_size(axis)
    pairs = [(i, i + by) for i in range(length) if 0 <= i + by < length]
    return lax.ppermute(x, axis, pairs)


def exchange_matrix(size):
    rows = lax.broadcasted_iota(jnp.int32, (size, size), 0)
    cols = lax.broadcasted_iota(jnp.int32, (size, size), 1)
    return jnp.where(rows + cols == size - 1, 1.0, 0.0).astype(jnp.bfloat16)


def reversed_rows(flip, block):
    return jnp.dot(flip, block, preferred_element_type=jnp.float32).astype(jnp.bfloat16)


def prepare_kernel(gate_ref, value_ref, grad_ref, mixed_ref, reversed_ref):
    flip = exchange_matrix(value_ref.shape[0])
    mixed_ref[...] = (
        gate_ref[...].astype(jnp.float32) * grad_ref[...].astype(jnp.float32)
    ).astype(jnp.bfloat16)
    reversed_ref[...] = reversed_rows(flip, value_ref[...])


def prepare(gate_rows, value_rows, grad_rows):
    shape = jax.ShapeDtypeStruct(gate_rows.shape, jnp.bfloat16)
    return pl.pallas_call(
        prepare_kernel,
        out_shape=(shape, shape),
        name="prepare",
        cost_estimate=pl.CostEstimate(flops=40_000_000, bytes_accessed=1_400_000, transcendentals=0),
    )(gate_rows, value_rows, grad_rows)


def toeplitz_kernel(taps_ref, matrix_ref):
    groups, tok_rows, width = matrix_ref.shape
    taps = taps_ref[...].astype(jnp.float32)
    padded = jnp.concatenate([taps, jnp.zeros((groups, width - taps.shape[1]), jnp.float32)], axis=1)
    for g in range(groups):
        spread = jnp.broadcast_to(padded[g : g + 1, :], (tok_rows, width))
        sheared = pltpu.roll(spread, 0, 1, stride=1, stride_axis=0)
        matrix_ref[g] = sheared.astype(jnp.bfloat16)


def toeplitz(taps, tok_rows):
    groups, lag_count = taps.shape
    step = 8
    width = lag_count + tok_rows
    return pl.pallas_call(
        toeplitz_kernel,
        grid=(groups // step,),
        in_specs=[pl.BlockSpec((step, lag_count), lambda i: (i, 0))],
        out_specs=pl.BlockSpec((step, tok_rows, width), lambda i: (i, 0, 0)),
        out_shape=jax.ShapeDtypeStruct((groups, tok_rows, width), jnp.bfloat16),
        name="toeplitz",
        cost_estimate=pl.CostEstimate(flops=12_000_000_000, bytes_accessed=6_400_000, transcendentals=0),
    )(taps)


def lane_group(shape, group_size):
    return lax.broadcasted_iota(jnp.int32, shape, len(shape) - 1) // group_size


def pair_kernel(group_size, lag_count, *refs):
    *block_refs, out_ref = refs
    spans = len(block_refs) // 3
    tok_rows = block_refs[0].shape[0]
    per_chunk = LANES // group_size
    owner = lane_group((tok_rows, LANES), group_size)
    width = 3 * tok_rows
    sums = [[None] * (2 * spans + 1) for _ in range(per_chunk)]
    for k in range(spans):
        grad = block_refs[3 * k][...]
        right = jnp.concatenate([block_refs[3 * k + 1][...], block_refs[3 * k + 2][...]], axis=0)
        left = jnp.concatenate(
            [jnp.where(owner == g, grad, jnp.zeros_like(grad)) for g in range(per_chunk)], axis=0
        )
        paired = lax.dot_general(
            left, right, (((1,), (1,)), ((), ())), preferred_element_type=jnp.float32
        )
        for g in range(per_chunk):
            mine = paired[g * tok_rows : (g + 1) * tok_rows]
            wide = jnp.concatenate([mine, jnp.zeros((tok_rows, tok_rows), jnp.float32)], axis=1)
            sheared = pltpu.roll(wide, 1, 1, stride=1, stride_axis=0)
            total = jnp.sum(sheared, axis=0, keepdims=True)
            for part in range(3):
                piece = total[:, part * tok_rows : (part + 1) * tok_rows]
                held = sums[g][2 * k + part]
                sums[g][2 * k + part] = piece if held is None else held + piece
    lag_blocks = lag_count // tok_rows
    for g in range(per_chunk):
        out_ref[0, g : g + 1, :] = jnp.concatenate(sums[g][1 : 1 + lag_blocks], axis=1)


def pair_sums(triples, group_size, lag_count):
    tok_rows, channels = triples[0][0].shape
    flat = [block for triple in triples for block in triple]
    chunks = channels // LANES
    per_chunk = LANES // group_size
    spec = pl.BlockSpec((tok_rows, LANES), lambda i: (0, i))
    out = pl.pallas_call(
        lambda *refs: pair_kernel(group_size, lag_count, *refs),
        grid=(chunks,),
        in_specs=[spec] * len(flat),
        out_specs=pl.BlockSpec((1, per_chunk, lag_count), lambda i: (i, 0, 0)),
        out_shape=jax.ShapeDtypeStruct((chunks, per_chunk, lag_count), jnp.float32),
        name="pair_sums",
        cost_estimate=pl.CostEstimate(flops=12_000_000_000, bytes_accessed=2_500_000, transcendentals=0),
    )(*flat)
    return out.reshape(chunks * per_chunk, lag_count)


def convolve_kernel(group_size, spans, *refs):
    matrix_ref, gate_ref, grad_ref = refs[:3]
    value_refs = refs[3 : 3 + spans]
    mixed_refs = refs[3 + spans : 3 + 2 * spans]
    output_ref, grad_gate_ref, grad_conv_ref = refs[3 + 2 * spans :]
    per_chunk, tok_rows, width = matrix_ref.shape
    flip = exchange_matrix(tok_rows)
    right = jnp.concatenate(
        [
            jnp.concatenate([value_refs[m][...], mixed_refs[m][...]], axis=1)
            for m in range(spans)
        ],
        axis=0,
    )
    left = matrix_ref[...].reshape(per_chunk * tok_rows, width)
    product = jnp.dot(left, right, preferred_element_type=jnp.float32)
    owner = lane_group((tok_rows, 2 * LANES), group_size) % per_chunk
    chosen = product[:tok_rows]
    for g in range(1, per_chunk):
        chosen = jnp.where(owner == g, product[g * tok_rows : (g + 1) * tok_rows], chosen)
    convolved = chosen[:, :LANES]
    gate = jnp.dot(flip, gate_ref[...], preferred_element_type=jnp.float32)
    grad = jnp.dot(flip, grad_ref[...], preferred_element_type=jnp.float32)
    output_ref[...] = reversed_rows(flip, (gate * convolved).astype(jnp.bfloat16))
    grad_gate_ref[...] = reversed_rows(flip, (grad * convolved).astype(jnp.bfloat16))
    grad_conv_ref[...] = chosen[:, LANES:].astype(jnp.bfloat16)


def convolve(matrix, gate_rows, grad_rows, values, mixed, group_size):
    groups, tok_rows, width = matrix.shape
    channels = gate_rows.shape[1]
    chunks = channels // LANES
    per_chunk = LANES // group_size
    spec = pl.BlockSpec((tok_rows, LANES), lambda i: (0, i))
    shape = jax.ShapeDtypeStruct((tok_rows, channels), jnp.bfloat16)
    spans = len(values)
    return pl.pallas_call(
        lambda *refs: convolve_kernel(group_size, spans, *refs),
        grid=(chunks,),
        in_specs=[pl.BlockSpec((per_chunk, tok_rows, width), lambda i: (i, 0, 0))]
        + [spec] * (2 + 2 * spans),
        out_specs=[spec] * 3,
        out_shape=[shape] * 3,
        name="convolve",
        cost_estimate=pl.CostEstimate(flops=12_000_000_000, bytes_accessed=10_500_000, transcendentals=0),
    )(matrix, gate_rows, grad_rows, *values, *mixed)


def owner_sums(partial_value):
    groups, lag_count = partial_value.shape
    members = lax.axis_size("dp") * lax.axis_size("ctx")
    own = lag_count // members
    pieces = partial_value.reshape(groups, members, own).transpose(1, 0, 2)
    pieces = pieces.reshape(members, groups * own)
    met = lax.all_to_all(pieces, ("dp", "ctx"), 0, 0, tiled=True)
    return jnp.sum(met, axis=0).reshape(groups, own)


def shards(gate_input, conv_input, grad_output, kernel):
    tok_rows = gate_input.shape[1]
    channels = gate_input.shape[2]
    groups = kernel.shape[0]
    group_size = channels // groups
    lag_count = kernel.shape[1]
    lag_blocks = lag_count // tok_rows
    blocks = lax.axis_size("ctx")
    gate_rows, value_rows, grad_rows = gate_input[0], conv_input[0], grad_output[0]

    mixed_rows, reversed_values = prepare(gate_rows, value_rows, grad_rows)
    values, mixed = [reversed_values], [mixed_rows]
    for _ in range(lag_blocks):
        values.append(passed_along(values[-1], "ctx", 1))
        mixed.append(passed_along(mixed[-1], "ctx", -1))
    matrix = toeplitz(kernel, tok_rows)
    triples = [(mixed[k], values[k], values[k + 1]) for k in range(lag_blocks // 2 + 1)]
    partial_value = pair_sums(triples, group_size, lag_count)
    summed = owner_sums(partial_value)
    output, grad_gate, grad_conv = convolve(
        matrix, gate_rows, grad_rows, values, mixed, group_size
    )
    grad_kernel = summed / math.sqrt(lax.axis_size("dp") * tok_rows * blocks)
    return (output[None], grad_gate[None], grad_conv[None], grad_kernel)


def solution(mesh):
    return jax.shard_map(
        shards,
        mesh=mesh,
        in_specs=(P("dp", "ctx", "ch"), P("dp", "ctx", "ch"), P("dp", "ctx", "ch"), P("ch", None)),
        out_specs=(
            P("dp", "ctx", "ch"),
            P("dp", "ctx", "ch"),
            P("dp", "ctx", "ch"),
            P("ch", ("dp", "ctx")),
        ),
        check_vma=False,
    )
```

time: 639 us -> 99.8 us (0.16)
  waiting for transfers between devices: 411 us -> 11 us
  local copies, waits for them, and re-layouts: 113 us -> 6.53 us
  Pallas kernels: 0 us -> 23.6 us
  other arithmetic: 17.1 us -> 0.16 us
  between operations: 14.9 us -> 0.86 us
  starting transfers between devices: 70 us -> 56.2 us
  matrix products: 10.7 us -> 0 us
    unnamed x2 -> x0, waiting for transfers between devices: 398 us -> none
    reshape x6 -> x0, local copies, waits for them, and re-layouts: 46.7 us -> none  [toeplitz(): return tiled.reshape(groups, tok_rows, 2 * tok_rows - 1)[:, :, :tok_rows]]
    ppermute x10, starting transfers between devices: 69.9 us -> 29.4 us  [passed_along(): return lax.ppermute(x, axis, pairs)]
    all_to_all x0 -> x1, starting transfers between devices: none -> 26.9 us  [owner_sums(): met = lax.all_to_all(pieces, ('dp', 'ctx'), 0, 0, tiled=True)]
    pallas_call x0 -> x4, Pallas kernels: none -> 23.6 us  [the longest x1 9.03 us: convolve(): pl.pallas_call(lambda *refs: convolve_kernel(group_size, spans, *refs), g...]
    while x57 -> x0, local copies, waits for them, and re-layouts: 20.7 us -> none
    slice x30 -> x0, local copies, waits for them, and re-layouts: 14.4 us -> none  [the longest x5 6.46 us: toeplitz(): return tiled.reshape(groups, tok_rows, 2 * tok_rows - 1)[:, :, :tok_rows]]
    ppermute x10, waiting for transfers between devices: 12.8 us -> 0.06 us  [passed_along(): return lax.ppermute(x, axis, pairs)]
  transfers between devices with their start and end apart: 11 -> 11, of which waited for: 2 -> 1; matrix products, arithmetic and copies ran while one was open for 10% -> 5% of each run, Pallas kernels for 0% -> 13%
where the time goes in v1:
time: 99.8 us; the launch traced here: 98.4 us
  starting transfers between devices  56.2 us (56%)
  Pallas kernels  23.6 us (24%)
  waiting for transfers between devices  11 us (11%)
  local copies, waits for them, and re-layouts  6.53 us (7%)
    ppermute x10, starting transfers between devices, passed_along(): return lax.ppermute(x, axis, pairs)  29.4 us
    all_to_all x1, starting transfers between devices, owner_sums(): met = lax.all_to_all(pieces, ('dp', 'ctx'), 0, 0, tiled=True)  26.9 us
    all_to_all x1, waiting for transfers between devices, owner_sums(): met = lax.all_to_all(pieces, ('dp', 'ctx'), 0, 0, tiled=True)  10.9 us
    pallas_call x1, Pallas kernels, convolve(): pl.pallas_call(lambda *refs: convolve_kernel(group_size, spans, *refs), g...  9.03 us
    pallas_call x1, Pallas kernels, pair_sums(): pl.pallas_call(lambda *refs: pair_kernel(group_size, lag_count, *refs), g...  7.69 us
    pallas_call x1, Pallas kernels, toeplitz(): pl.pallas_call(toeplitz_kernel, grid=(groups // step,), in_specs=[pl.Bloc...  4.74 us
    another operation x1, local copies, waits for them, and re-layouts, owner_sums(): pieces = partial_value.reshape(groups, members, own).transpose(1, 0, 2)  2.92 us
    pallas_call x1, Pallas kernels, prepare(): pl.pallas_call(prepare_kernel, out_shape=(shape, shape), name='prepare',...  2.17 us
  transfers between devices with their start and end apart: 11, of which 1 were waited for; matrix products, arithmetic and copies ran while one was open for 5% of the time, Pallas kernels for 13%

profile of v1, /device:TPU:24, one launch (start us, length us, event | category | flops | bytes accessed | tf_op | source)
XLA Modules:
  0.0 98.4 jit_solution(3693810621849393000)
XLA Ops:
  0.6 2.2 %prepare.1 = (bf16[128,1024]{1,0:T(8,128)(2,1)}, bf16[128,1024]{1,0:T(8,128)(2,1)}) custom-call(bf16[128,1024]{1,0:T(8,128)(2,1)} %bitcast.11, bf16[128,1024]{1,0:T(8,128)(2,1)} %bitcast.10, bf16[128,1024]{1,0:T(8,128)(2,1)} %bitcast.13), custom_call_target="tpu_custom_call" | custom-call | flops 40000000 | bytes 1400000 | tf_op jit(solution)/shard_map/prepare/pallas_call | solution.py:39
  2.8 1.7 %collective-permute-start = (bf16[128,1024]{1,0:T(8,128)(2,1)}, bf16[128,1024]{1,0:T(8,128)(2,1)S(1)}, u32[]{:S(2)}, u32[]{:S(2)}) collective-permute-start(bf16[128,1024]{1,0:T(8,128)(2,1)} %get-tuple-element.9.refs_3_.refs_1_), channel_id=1, source_target_pairs={{0,4},{4,8},{8,12},{12,16},{16,20},{20,24},{24,28},{28,32},{32,36}... | collective-permute-start | bytes 786440 | tf_op jit(solution)/shard_map/ppermute | solution.py:16
  4.6 1.3 %collective-permute-start.5 = (bf16[128,1024]{1,0:T(8,128)(2,1)}, bf16[128,1024]{1,0:T(8,128)(2,1)S(1)}, u32[]{:S(2)}, u32[]{:S(2)}) collective-permute-start(bf16[128,1024]{1,0:T(8,128)(2,1)} %get-tuple-element.10.refs_9_.refs_0_), channel_id=1, source_target_pairs={{4,0},{8,4},{12,8},{16,12},{20,16},{24,20},{28,24},{32,28},{36,32}... | collective-permute-start | bytes 786440 | tf_op jit(solution)/shard_map/ppermute | solution.py:16
  5.9 0.0 collective-permute-done.refs_4_.refs_2_
  5.9 6.4 %collective-permute-start.1 = (bf16[128,1024]{1,0:T(8,128)(2,1)S(1)}, bf16[128,1024]{1,0:T(8,128)(2,1)S(1)}, u32[]{:S(2)}, u32[]{:S(2)}) collective-permute-start(bf16[128,1024]{1,0:T(8,128)(2,1)S(1)} %collective-permute-done.refs_4_.refs_2_), channel_id=1, source_target_pairs={{0,4},{4,8},{8,12},{12,16},{16,20},{20,24},{24,28},{28,32},{32,36}... | collective-permute-start | bytes 786440 | tf_op jit(solution)/shard_map/ppermute | solution.py:16
  12.3 0.0 collective-permute-done.5.refs_10_.refs_3_
  12.3 1.3 %collective-permute-start.6 = (bf16[128,1024]{1,0:T(8,128)(2,1)S(1)}, bf16[128,1024]{1,0:T(8,128)(2,1)S(1)}, u32[]{:S(2)}, u32[]{:S(2)}) collective-permute-start(bf16[128,1024]{1,0:T(8,128)(2,1)S(1)} %collective-permute-done.5.refs_10_.refs_3_), channel_id=1, source_target_pairs={{4,0},{8,4},{12,8},{16,12},{20,16},{24,20},{28,24},{32,28},{36,32}... | collective-permute-start | bytes 786440 | tf_op jit(solution)/shard_map/ppermute | solution.py:16
  13.6 0.0 collective-permute-done.1.refs_5_.refs_7_
  13.6 6.2 %collective-permute-start.2 = (bf16[128,1024]{1,0:T(8,128)(2,1)S(1)}, bf16[128,1024]{1,0:T(8,128)(2,1)S(1)}, u32[]{:S(2)}, u32[]{:S(2)}) collective-permute-start(bf16[128,1024]{1,0:T(8,128)(2,1)S(1)} %collective-permute-done.1.refs_5_.refs_7_), channel_id=1, source_target_pairs={{0,4},{4,8},{8,12},{12,16},{16,20},{20,24},{24,28},{28,32},{32,36}... | collective-permute-start | bytes 786440 | tf_op jit(solution)/shard_map/ppermute | solution.py:16
  19.8 0.0 collective-permute-done.6.refs_11_.refs_6_
  19.9 1.3 %collective-permute-start.7 = (bf16[128,1024]{1,0:T(8,128)(2,1)S(1)}, bf16[128,1024]{1,0:T(8,128)(2,1)}, u32[]{:S(2)}, u32[]{:S(2)}) collective-permute-start(bf16[128,1024]{1,0:T(8,128)(2,1)S(1)} %collective-permute-done.6.refs_11_.refs_6_), channel_id=1, source_target_pairs={{4,0},{8,4},{12,8},{16,12},{20,16},{24,20},{28,24},{32,28},{36,32}... | collective-permute-start | bytes 786440 | tf_op jit(solution)/shard_map/ppermute | solution.py:16
  21.2 0.0 collective-permute-done.2.refs_6_.refs_8_
  21.2 7.0 %collective-permute-start.3 = (bf16[128,1024]{1,0:T(8,128)(2,1)S(1)}, bf16[128,1024]{1,0:T(8,128)(2,1)}, u32[]{:S(2)}, u32[]{:S(2)}) collective-permute-start(bf16[128,1024]{1,0:T(8,128)(2,1)S(1)} %collective-permute-done.2.refs_6_.refs_8_), channel_id=1, source_target_pairs={{0,4},{4,8},{8,12},{12,16},{16,20},{20,24},{24,28},{28,32},{32,36}... | collective-permute-start | bytes 786440 | tf_op jit(solution)/shard_map/ppermute | solution.py:16
  28.2 0.0 collective-permute-done.7.refs_12_
  28.2 1.3 %collective-permute-start.8 = (bf16[128,1024]{1,0:T(8,128)(2,1)}, bf16[128,1024]{1,0:T(8,128)(2,1)}, u32[]{:S(2)}, u32[]{:S(2)}) collective-permute-start(bf16[128,1024]{1,0:T(8,128)(2,1)} %collective-permute-done.7.refs_12_), channel_id=1, source_target_pairs={{4,0},{8,4},{12,8},{16,12},{20,16},{24,20},{28,24},{32,28},{36,32}... | collective-permute-start | bytes 786440 | tf_op jit(solution)/shard_map/ppermute | solution.py:16
  29.6 7.7 %pair_sums.1 = f32[8,4,640]{2,1,0:T(4,128)} custom-call(bf16[128,1024]{1,0:T(8,128)(2,1)} %get-tuple-element.10.refs_9_.refs_0_, bf16[128,1024]{1,0:T(8,128)(2,1)} %get-tuple-element.9.refs_3_.refs_1_, bf16[128,1024]{1,0:T(8,128)(2,1)} %copy-done, bf16[128,1024]{1,0:T(8,128)(2,1)} %copy-done.1, bf16[128,1024]{1,0:T(8,128)(2,1)} %copy-done, ...), custom_call_target="tpu_custom_call" | custom-call | flops 12000000000 | bytes 2500000 | tf_op jit(solution)/shard_map/pair_sums/pallas_call | solution.py:113
  37.2 2.9 %reshape_reshape.3 = f32[32,128,5]{2,1,0:T(8,128)S(1)} reshape(f32[8,4,640]{2,1,0:T(4,128)} %pair_sums.1) | data formatting | bytes 163840 | tf_op jit(solution)/shard_map/reshape;reshape | solution.py:177
  40.2 0.6 copy.10
  40.8 0.8 copy.11
  41.6 26.9 %all-to-all-start = ((f32[128,1,160]{2,1,0:T(1,128)}), f32[128,1,160]{2,1,0:T(1,128)S(1)}, u32[]{:S(2)}, u32[]{:S(2)}) async-start(f32[128,1,160]{2,1,0:T(1,128)} %copy.11), calls=%async_computation | async-start | bytes 262144 | tf_op jit(solution)/shard_map/all_to_all | solution.py:179
  68.4 0.0 collective-permute-done.3.refs_7_
  68.5 1.5 %collective-permute-start.4 = (bf16[128,1024]{1,0:T(8,128)(2,1)}, bf16[128,1024]{1,0:T(8,128)(2,1)S(1)}, u32[]{:S(2)}, u32[]{:S(2)}) collective-permute-start(bf16[128,1024]{1,0:T(8,128)(2,1)} %collective-permute-done.3.refs_7_), channel_id=1, source_target_pairs={{0,4},{4,8},{8,12},{12,16},{16,20},{20,24},{24,28},{28,32},{32,36}... | collective-permute-start | bytes 786440 | tf_op jit(solution)/shard_map/ppermute | solution.py:16
  70.0 0.0 collective-permute-done.8.refs_13_
  70.0 1.3 %collective-permute-start.9 = (bf16[128,1024]{1,0:T(8,128)(2,1)}, bf16[128,1024]{1,0:T(8,128)(2,1)S(1)}, u32[]{:S(2)}, u32[]{:S(2)}) collective-permute-start(bf16[128,1024]{1,0:T(8,128)(2,1)} %collective-permute-done.8.refs_13_), channel_id=1, source_target_pairs={{4,0},{8,4},{12,8},{16,12},{20,16},{24,20},{28,24},{32,28},{36,32}... | collective-permute-start | bytes 786440 | tf_op jit(solution)/shard_map/ppermute | solution.py:16
  71.3 4.7 %toeplitz.1.refs_0_ = bf16[32,128,768]{2,1,0:T(8,128)(2,1)} custom-call(bf16[32,640]{1,0:T(8,128)(2,1)} %taps_ref.1), custom_call_target="tpu_custom_call" | custom-call | flops 12000000000 | bytes 6400000 | tf_op jit(solution)/shard_map/toeplitz/pallas_call | solution.py:61
  76.1 10.9 %all-to-all-done = f32[128,1,160]{2,1,0:T(1,128)S(1)} async-done(((f32[128,1,160]{2,1,0:T(1,128)}), f32[128,1,160]{2,1,0:T(1,128)S(1)}, u32[]{:S(2)}, u32[]{:S(2)}) %all-to-all-start) | async-done | bytes 81952 | tf_op jit(solution)/shard_map/all_to_all | solution.py:179
  87.0 0.2 reduce_sum.9
  87.1 0.1 div.10
  87.3 0.7 copy.12
  87.9 0.7 copy-done.5
  88.7 0.7 copy-done.6
  89.4 9.0 %convolve.1 = (bf16[128,1024]{1,0:T(8,128)(2,1)}, bf16[128,1024]{1,0:T(8,128)(2,1)}, bf16[128,1024]{1,0:T(8,128)(2,1)}) custom-call(bf16[32,128,768]{2,1,0:T(8,128)(2,1)} %toeplitz.1.refs_0_, bf16[128,1024]{1,0:T(8,128)(2,1)} %bitcast.12, bf16[128,1024]{1,0:T(8,128)(2,1)} %bitcast.14, bf16[128,1024]{1,0:T(8,128)(2,1)} %get-tuple-element.9.refs_3_.refs_1_, ...), custom_call_target="tpu_custom_call" | custom-call | flops 12000000000 | bytes 10500000 | tf_op jit(solution)/shard_map/convolve/pallas_call | solution.py:161
  (16 shorter events, 0.1 us)
Async XLA Ops:
  2.8 3.1 %collective-permute-start = (bf16[128,1024]{1,0:T(8,128)(2,1)}, bf16[128,1024]{1,0:T(8,128)(2,1)S(1)}, u32[]{:S(2)}, u32[]{:S(2)}) collective-permute-start(bf16[128,1024]{1,0:T(8,128)(2,1)} %get-tuple-element.9.refs_3_.refs_1_), channel_id=1, source_target_pairs={{0,4},{4,8},{8,12},{12,16},{16,20},{20,24},{24,28},{28,32},{32,36}... | collective-permute-start | bytes 786440 | tf_op jit(solution)/shard_map/ppermute | solution.py:16
  4.6 7.7 %collective-permute-start.5 = (bf16[128,1024]{1,0:T(8,128)(2,1)}, bf16[128,1024]{1,0:T(8,128)(2,1)S(1)}, u32[]{:S(2)}, u32[]{:S(2)}) collective-permute-start(bf16[128,1024]{1,0:T(8,128)(2,1)} %get-tuple-element.10.refs_9_.refs_0_), channel_id=1, source_target_pairs={{4,0},{8,4},{12,8},{16,12},{20,16},{24,20},{28,24},{32,28},{36,32}... | collective-permute-start | bytes 786440 | tf_op jit(solution)/shard_map/ppermute | solution.py:16
  5.9 23.6 %copy-start = (bf16[128,1024]{1,0:T(8,128)(2,1)}, bf16[128,1024]{1,0:T(8,128)(2,1)S(1)}, u32[]{:S(2)}) copy-start(bf16[128,1024]{1,0:T(8,128)(2,1)S(1)} %collective-permute-done.refs_4_.refs_2_) | copy-start | bytes 786436
  5.9 7.7 %collective-permute-start.1 = (bf16[128,1024]{1,0:T(8,128)(2,1)S(1)}, bf16[128,1024]{1,0:T(8,128)(2,1)S(1)}, u32[]{:S(2)}, u32[]{:S(2)}) collective-permute-start(bf16[128,1024]{1,0:T(8,128)(2,1)S(1)} %collective-permute-done.refs_4_.refs_2_), channel_id=1, source_target_pairs={{0,4},{4,8},{8,12},{12,16},{16,20},{20,24},{24,28},{28,32},{32,36}... | collective-permute-start | bytes 786440 | tf_op jit(solution)/shard_map/ppermute | solution.py:16
  12.3 17.2 %copy-start.1 = (bf16[128,1024]{1,0:T(8,128)(2,1)}, bf16[128,1024]{1,0:T(8,128)(2,1)S(1)}, u32[]{:S(2)}) copy-start(bf16[128,1024]{1,0:T(8,128)(2,1)S(1)} %collective-permute-done.5.refs_10_.refs_3_) | copy-start | bytes 786436
  12.3 7.6 %collective-permute-start.6 = (bf16[128,1024]{1,0:T(8,128)(2,1)S(1)}, bf16[128,1024]{1,0:T(8,128)(2,1)S(1)}, u32[]{:S(2)}, u32[]{:S(2)}) collective-permute-start(bf16[128,1024]{1,0:T(8,128)(2,1)S(1)} %collective-permute-done.5.refs_10_.refs_3_), channel_id=1, source_target_pairs={{4,0},{8,4},{12,8},{16,12},{20,16},{24,20},{28,24},{32,28},{36,32}... | collective-permute-start | bytes 786440 | tf_op jit(solution)/shard_map/ppermute | solution.py:16
  13.6 15.9 %copy-start.2 = (bf16[128,1024]{1,0:T(8,128)(2,1)}, bf16[128,1024]{1,0:T(8,128)(2,1)S(1)}, u32[]{:S(2)}) copy-start(bf16[128,1024]{1,0:T(8,128)(2,1)S(1)} %collective-permute-done.1.refs_5_.refs_7_) | copy-start | bytes 786436
  13.6 7.6 %collective-permute-start.2 = (bf16[128,1024]{1,0:T(8,128)(2,1)S(1)}, bf16[128,1024]{1,0:T(8,128)(2,1)S(1)}, u32[]{:S(2)}, u32[]{:S(2)}) collective-permute-start(bf16[128,1024]{1,0:T(8,128)(2,1)S(1)} %collective-permute-done.1.refs_5_.refs_7_), channel_id=1, source_target_pairs={{0,4},{4,8},{8,12},{12,16},{16,20},{20,24},{24,28},{28,32},{32,36}... | collective-permute-start | bytes 786440 | tf_op jit(solution)/shard_map/ppermute | solution.py:16
  19.9 9.7 %copy-start.3 = (bf16[128,1024]{1,0:T(8,128)(2,1)}, bf16[128,1024]{1,0:T(8,128)(2,1)S(1)}, u32[]{:S(2)}) copy-start(bf16[128,1024]{1,0:T(8,128)(2,1)S(1)} %collective-permute-done.6.refs_11_.refs_6_) | copy-start | bytes 786436
  19.9 8.4 %collective-permute-start.7 = (bf16[128,1024]{1,0:T(8,128)(2,1)S(1)}, bf16[128,1024]{1,0:T(8,128)(2,1)}, u32[]{:S(2)}, u32[]{:S(2)}) collective-permute-start(bf16[128,1024]{1,0:T(8,128)(2,1)S(1)} %collective-permute-done.6.refs_11_.refs_6_), channel_id=1, source_target_pairs={{4,0},{8,4},{12,8},{16,12},{20,16},{24,20},{28,24},{32,28},{36,32}... | collective-permute-start | bytes 786440 | tf_op jit(solution)/shard_map/ppermute | solution.py:16
  21.2 8.4 %copy-start.4 = (bf16[128,1024]{1,0:T(8,128)(2,1)}, bf16[128,1024]{1,0:T(8,128)(2,1)S(1)}, u32[]{:S(2)}) copy-start(bf16[128,1024]{1,0:T(8,128)(2,1)S(1)} %collective-permute-done.2.refs_6_.refs_8_) | copy-start | bytes 786436
  21.2 47.3 %collective-permute-start.3 = (bf16[128,1024]{1,0:T(8,128)(2,1)S(1)}, bf16[128,1024]{1,0:T(8,128)(2,1)}, u32[]{:S(2)}, u32[]{:S(2)}) collective-permute-start(bf16[128,1024]{1,0:T(8,128)(2,1)S(1)} %collective-permute-done.2.refs_6_.refs_8_), channel_id=1, source_target_pairs={{0,4},{4,8},{8,12},{12,16},{16,20},{20,24},{24,28},{28,32},{32,36}... | collective-permute-start | bytes 786440 | tf_op jit(solution)/shard_map/ppermute | solution.py:16
  28.2 41.8 %collective-permute-start.8 = (bf16[128,1024]{1,0:T(8,128)(2,1)}, bf16[128,1024]{1,0:T(8,128)(2,1)}, u32[]{:S(2)}, u32[]{:S(2)}) collective-permute-start(bf16[128,1024]{1,0:T(8,128)(2,1)} %collective-permute-done.7.refs_12_), channel_id=1, source_target_pairs={{4,0},{8,4},{12,8},{16,12},{20,16},{24,20},{28,24},{32,28},{36,32}... | collective-permute-start | bytes 786440 | tf_op jit(solution)/shard_map/ppermute | solution.py:16
  41.6 45.4 %all-to-all-start = ((f32[128,1,160]{2,1,0:T(1,128)}), f32[128,1,160]{2,1,0:T(1,128)S(1)}, u32[]{:S(2)}, u32[]{:S(2)}) async-start(f32[128,1,160]{2,1,0:T(1,128)} %copy.11), calls=%async_computation | async-start | bytes 262144 | tf_op jit(solution)/shard_map/all_to_all | solution.py:179
  68.5 19.5 %collective-permute-start.4 = (bf16[128,1024]{1,0:T(8,128)(2,1)}, bf16[128,1024]{1,0:T(8,128)(2,1)S(1)}, u32[]{:S(2)}, u32[]{:S(2)}) collective-permute-start(bf16[128,1024]{1,0:T(8,128)(2,1)} %collective-permute-done.3.refs_7_), channel_id=1, source_target_pairs={{0,4},{4,8},{8,12},{12,16},{16,20},{20,24},{24,28},{28,32},{32,36}... | collective-permute-start | bytes 786440 | tf_op jit(solution)/shard_map/ppermute | solution.py:16
  70.0 17.9 %collective-permute-start.9 = (bf16[128,1024]{1,0:T(8,128)(2,1)}, bf16[128,1024]{1,0:T(8,128)(2,1)S(1)}, u32[]{:S(2)}, u32[]{:S(2)}) collective-permute-start(bf16[128,1024]{1,0:T(8,128)(2,1)} %collective-permute-done.8.refs_13_), channel_id=1, source_target_pairs={{4,0},{8,4},{12,8},{16,12},{20,16},{24,20},{28,24},{32,28},{36,32}... | collective-permute-start | bytes 786440 | tf_op jit(solution)/shard_map/ppermute | solution.py:16
  87.9 0.7 copy-start.5
  88.7 0.7 copy-start.6

commit v2 on v1

v2 whole, which is shorter than its diff:
```python
import math

import jax
import jax.numpy as jnp
from jax import lax
from jax.experimental import pallas as pl
from jax.experimental.pallas import tpu as pltpu
from jax.sharding import PartitionSpec as P

LANES = 128
SCOPED = 16 * 1024 * 1024


def exchange_matrix(size):
    rows = lax.broadcasted_iota(jnp.int32, (size, size), 0)
    cols = lax.broadcasted_iota(jnp.int32, (size, size), 1)
    return jnp.where(rows + cols == size - 1, 1.0, 0.0).astype(jnp.bfloat16)


def reversed_rows(flip, block):
    return jnp.dot(flip, block, preferred_element_type=jnp.float32).astype(jnp.bfloat16)


def prepare_kernel(gate_ref, value_ref, grad_ref, mixed_ref, reversed_ref):
    flip = exchange_matrix(value_ref.shape[0])
    mixed_ref[...] = (
        gate_ref[...].astype(jnp.float32) * grad_ref[...].astype(jnp.float32)
    ).astype(jnp.bfloat16)
    reversed_ref[...] = reversed_rows(flip, value_ref[...])


def prepare(gate_rows, value_rows, grad_rows):
    shape = jax.ShapeDtypeStruct(gate_rows.shape, jnp.bfloat16)
    return pl.pallas_call(
        prepare_kernel,
        out_shape=(shape, shape),
        name="prepare",
        compiler_params=pltpu.CompilerParams(vmem_limit_bytes=SCOPED),
        cost_estimate=pl.CostEstimate(flops=40_000_000, bytes_accessed=1_400_000, transcendentals=0),
    )(gate_rows, value_rows, grad_rows)


def toeplitz_kernel(taps_ref, matrix_ref):
    groups, tok_rows, width = matrix_ref.shape
    taps = taps_ref[...].astype(jnp.float32)
    padded = jnp.concatenate([taps, jnp.zeros((groups, width - taps.shape[1]), jnp.float32)], axis=1)
    for g in range(groups):
        spread = jnp.broadcast_to(padded[g : g + 1, :], (tok_rows, width))
        sheared = pltpu.roll(spread, 0, 1, stride=1, stride_axis=0)
        matrix_ref[g] = sheared.astype(jnp.bfloat16)


def toeplitz(taps, tok_rows):
    groups, lag_count = taps.shape
    step = 8
    width = lag_count + tok_rows
    return pl.pallas_call(
        toeplitz_kernel,
        grid=(groups // step,),
        in_specs=[pl.BlockSpec((step, lag_count), lambda i: (i, 0))],
        out_specs=pl.BlockSpec((step, tok_rows, width), lambda i: (i, 0, 0)),
        out_shape=jax.ShapeDtypeStruct((groups, tok_rows, width), jnp.bfloat16),
        name="toeplitz",
        cost_estimate=pl.CostEstimate(flops=12_000_000_000, bytes_accessed=6_400_000, transcendentals=0),
    )(taps)


def lane_group(shape, group_size):
    return lax.broadcasted_iota(jnp.int32, shape, len(shape) - 1) // group_size


def parity_select(parity, even, odd):
    return jnp.where(parity == 0, even, odd)


def lag_window(left_block, right_block, owner, per_chunk):
    tok_rows = left_block.shape[0]
    left = jnp.concatenate(
        [jnp.where(owner == g, left_block, jnp.zeros_like(left_block)) for g in range(per_chunk)],
        axis=0,
    )
    paired = lax.dot_general(
        left, right_block, (((1,), (1,)), ((), ())), preferred_element_type=jnp.float32
    )
    halves = []
    for g in range(per_chunk):
        mine = paired[g * tok_rows : (g + 1) * tok_rows]
        wide = jnp.concatenate([mine, jnp.zeros_like(mine)], axis=1)
        sheared = pltpu.roll(wide, 1, 1, stride=1, stride_axis=0)
        total = jnp.sum(sheared, axis=0, keepdims=True)
        halves.append((total[:, :tok_rows], total[:, tok_rows:]))
    return halves


def gathered_windows(windows, lag_blocks, per_chunk, tok_rows):
    rows = []
    for g in range(per_chunk):
        pieces = []
        for piece in range(lag_blocks):
            held = jnp.zeros((1, tok_rows), jnp.float32)
            if piece in windows:
                held = held + windows[piece][g][1]
            if piece + 1 in windows:
                held = held + windows[piece + 1][g][0]
            pieces.append(held)
        rows.append(jnp.concatenate(pieces, axis=1))
    return jnp.concatenate(rows, axis=0)


def near_kernel(group_size, parity_ref, mixed, mixed_swap, mixed_one, value, value_one, out_ref):
    tok_rows = mixed.shape[0]
    per_chunk, lag_count = out_ref.shape[1:]
    owner = lane_group((tok_rows, LANES), group_size)
    parity = parity_ref[0]
    second = parity_select(parity, value[...], value_one[...])
    windows = {
        0: lag_window(mixed[...], value[...], owner, per_chunk),
        2: lag_window(mixed[...], value_one[...], owner, per_chunk),
        4: lag_window(mixed_one[...], value_one[...], owner, per_chunk),
        1: lag_window(mixed_swap[...], second, owner, per_chunk),
    }
    out_ref[0] = gathered_windows(windows, lag_count // tok_rows, per_chunk, tok_rows)


def far_kernel(
    group_size, parity_ref, near_ref, mixed_swap, mixed_swap_one, value_one, value_two, out_ref, held_ref
):
    step = pl.program_id(0)
    tok_rows = mixed_swap.shape[0]
    chunks, per_chunk, lag_count = held_ref.shape
    owner = lane_group((tok_rows, LANES), group_size)
    parity = parity_ref[0]
    third = parity_select(parity, value_one[...], value_two[...])
    fifth = parity_select(parity, mixed_swap[...], mixed_swap_one[...])
    windows = {
        3: lag_window(mixed_swap[...], third, owner, per_chunk),
        5: lag_window(fifth, value_two[...], owner, per_chunk),
    }
    held_ref[step] = near_ref[0] + gathered_windows(
        windows, lag_count // tok_rows, per_chunk, tok_rows
    )

    @pl.when(step == chunks - 1)
    def _():
        groups = chunks * per_chunk
        members = out_ref.shape[0]
        own = lag_count // members
        sums = jnp.concatenate([held_ref[i] for i in range(chunks)], axis=0)
        high = sums.astype(jnp.bfloat16)
        rest = sums - high.astype(jnp.float32)
        middle = rest.astype(jnp.bfloat16)
        low = (rest - middle.astype(jnp.float32)).astype(jnp.bfloat16)
        lags = lax.broadcasted_iota(jnp.int32, (lag_count, lag_count), 0)
        cols = lax.broadcasted_iota(jnp.int32, (lag_count, lag_count), 1)
        picks = jnp.where(lags == own * (cols % members) + cols // members, 1.0, 0.0)
        split = jnp.dot(
            jnp.concatenate([high, middle, low], axis=0),
            picks.astype(jnp.bfloat16),
            preferred_element_type=jnp.float32,
        )
        moved = split[:groups] + split[groups : 2 * groups] + split[2 * groups :]
        out_ref[:, 0, :] = jnp.concatenate(
            [moved[:, r * members : (r + 1) * members].T for r in range(own)], axis=1
        )


def pair_sums(parity, mixed, values, group_size, lag_count, members):
    tok_rows, channels = values["own"].shape
    chunks = channels // LANES
    per_chunk = LANES // group_size
    groups = chunks * per_chunk
    own = lag_count // members
    spec = pl.BlockSpec((tok_rows, LANES), lambda i: (0, i))
    scalar = pl.BlockSpec(memory_space=pltpu.SMEM)
    part = pl.BlockSpec((1, per_chunk, lag_count), lambda i: (i, 0, 0))
    near = pl.pallas_call(
        lambda *refs: near_kernel(group_size, *refs),
        grid=(chunks,),
        in_specs=[scalar] + [spec] * 5,
        out_specs=part,
        out_shape=jax.ShapeDtypeStruct((chunks, per_chunk, lag_count), jnp.float32),
        name="pair_near",
        compiler_params=pltpu.CompilerParams(vmem_limit_bytes=SCOPED),
        cost_estimate=pl.CostEstimate(flops=8_000_000_000, bytes_accessed=1_500_000, transcendentals=0),
    )(parity, mixed["own"], mixed["swap"], mixed["one"], values["own"], values["one"])
    return pl.pallas_call(
        lambda *refs: far_kernel(group_size, *refs),
        grid=(chunks,),
        in_specs=[scalar, part] + [spec] * 4,
        out_specs=pl.BlockSpec((members, 1, groups * own), lambda i: (0, 0, 0)),
        out_shape=jax.ShapeDtypeStruct((members, 1, groups * own), jnp.float32),
        scratch_shapes=[pltpu.VMEM((chunks, per_chunk, lag_count), jnp.float32)],
        name="pair_far",
        compiler_params=pltpu.CompilerParams(vmem_limit_bytes=SCOPED),
        cost_estimate=pl.CostEstimate(flops=4_000_000_000, bytes_accessed=1_500_000, transcendentals=0),
    )(parity, near, mixed["swap"], mixed["swap_one"], values["one"], values["two"])


NAMES = ("own", "swap", "one", "swap_one", "two", "swap_two", "three")


def convolve_kernel(group_size, *refs):
    parity_ref, matrix_ref, gate_ref, grad_ref = refs[:4]
    value = {name: ref[...] for name, ref in zip(NAMES, refs[4:11])}
    mixed = {name: ref[...] for name, ref in zip(NAMES, refs[11:18])}
    output_ref, grad_gate_ref, grad_conv_ref = refs[18:]
    per_chunk, tok_rows, width = matrix_ref.shape
    parity = parity_ref[0]
    flip = exchange_matrix(tok_rows)
    values = [
        value["own"],
        parity_select(parity, value["swap_one"], value["swap"]),
        value["one"],
        parity_select(parity, value["swap_two"], value["swap_one"]),
        value["two"],
        parity_select(parity, value["three"], value["swap_two"]),
    ]
    mixes = [
        mixed["own"],
        parity_select(parity, mixed["swap"], mixed["swap_one"]),
        mixed["one"],
        parity_select(parity, mixed["swap_one"], mixed["swap_two"]),
        mixed["two"],
        parity_select(parity, mixed["swap_two"], mixed["three"]),
    ]
    right = jnp.concatenate(
        [jnp.concatenate([v, m], axis=1) for v, m in zip(values, mixes)], axis=0
    )
    left = matrix_ref[...].reshape(per_chunk * tok_rows, width)
    product = jnp.dot(left, right, preferred_element_type=jnp.float32)
    owner = lane_group((tok_rows, 2 * LANES), group_size) % per_chunk
    chosen = product[:tok_rows]
    for g in range(1, per_chunk):
        chosen = jnp.where(owner == g, product[g * tok_rows : (g + 1) * tok_rows], chosen)
    convolved = chosen[:, :LANES]
    gate = jnp.dot(flip, gate_ref[...], preferred_element_type=jnp.float32)
    grad = jnp.dot(flip, grad_ref[...], preferred_element_type=jnp.float32)
    output_ref[...] = reversed_rows(flip, (gate * convolved).astype(jnp.bfloat16))
    grad_gate_ref[...] = reversed_rows(flip, (grad * convolved).astype(jnp.bfloat16))
    grad_conv_ref[...] = chosen[:, LANES:].astype(jnp.bfloat16)


def convolve(parity, matrix, gate_rows, grad_rows, values, mixed, group_size):
    groups, tok_rows, width = matrix.shape
    channels = gate_rows.shape[1]
    chunks = channels // LANES
    per_chunk = LANES // group_size
    spec = pl.BlockSpec((tok_rows, LANES), lambda i: (0, i))
    scalar = pl.BlockSpec(memory_space=pltpu.SMEM)
    shape = jax.ShapeDtypeStruct((tok_rows, channels), jnp.bfloat16)
    return pl.pallas_call(
        lambda *refs: convolve_kernel(group_size, *refs),
        grid=(chunks,),
        in_specs=[scalar, pl.BlockSpec((per_chunk, tok_rows, width), lambda i: (i, 0, 0))]
        + [spec] * 16,
        out_specs=[spec] * 3,
        out_shape=[shape] * 3,
        name="convolve",
        compiler_params=pltpu.CompilerParams(vmem_limit_bytes=59 * 1024 * 1024),
        cost_estimate=pl.CostEstimate(flops=12_000_000_000, bytes_accessed=10_500_000, transcendentals=0),
    )(
        parity,
        matrix,
        gate_rows,
        grad_rows,
        *[values[name] for name in NAMES],
        *[mixed[name] for name in NAMES],
    )


def moved(x, by, lands):
    length = lax.axis_size("ctx")
    pairs = [(i, i + by) for i in range(length) if 0 <= i + by < length and lands(i + by)]
    return lax.ppermute(x, "ctx", pairs)


def swapped(x):
    return lax.ppermute(x, "ctx", [(i, i ^ 1) for i in range(lax.axis_size("ctx"))])


def shards(gate_input, conv_input, grad_output, kernel):
    tok_rows = gate_input.shape[1]
    channels = gate_input.shape[2]
    groups = kernel.shape[0]
    group_size = channels // groups
    lag_count = kernel.shape[1]
    blocks = lax.axis_size("ctx")
    members = lax.axis_size("dp") * blocks
    gate_rows, value_rows, grad_rows = gate_input[0], conv_input[0], grad_output[0]
    parity = lax.rem(lax.axis_index("ctx"), 2).reshape(1)
    anyone = lambda i: True
    even = lambda i: i % 2 == 0
    odd = lambda i: i % 2 == 1

    mixed_rows, reversed_values = prepare(gate_rows, value_rows, grad_rows)
    values, mixed = {"own": reversed_values}, {"own": mixed_rows}
    values["one"] = moved(values["own"], 2, anyone)
    mixed["one"] = moved(mixed["own"], -2, anyone)
    mixed["swap"] = swapped(mixed["own"])
    values["swap"] = swapped(values["own"])
    matrix = toeplitz(kernel, tok_rows)
    values["two"] = moved(values["one"], 2, anyone)
    mixed["two"] = moved(mixed["one"], -2, anyone)
    mixed["swap_one"] = swapped(mixed["one"])
    values["swap_one"] = swapped(values["one"])
    pieces = pair_sums(parity, mixed, values, group_size, lag_count, members)
    values["three"] = moved(values["two"], 1, even)
    mixed["three"] = moved(mixed["two"], -1, odd)
    values["swap_two"] = swapped(values["two"])
    mixed["swap_two"] = swapped(mixed["two"])
    met = lax.all_to_all(pieces, ("dp", "ctx"), 0, 0, tiled=True)
    output, grad_gate, grad_conv = convolve(
        parity, matrix, gate_rows, grad_rows, values, mixed, group_size
    )
    summed = jnp.sum(met, axis=(0, 1)).reshape(lag_count // members, groups).T
    grad_kernel = summed / math.sqrt(lax.axis_size("dp") * tok_rows * blocks)
    return (output[None], grad_gate[None], grad_conv[None], grad_kernel)


def solution(mesh):
    return jax.shard_map(
        shards,
        mesh=mesh,
        in_specs=(P("dp", "ctx", "ch"), P("dp", "ctx", "ch"), P("dp", "ctx", "ch"), P("ch", None)),
        out_specs=(
            P("dp", "ctx", "ch"),
            P("dp", "ctx", "ch"),
            P("dp", "ctx", "ch"),
            P("ch", ("dp", "ctx")),
        ),
        check_vma=False,
    )
```

time: 99.8 us -> 91.1 us (0.913)
  waiting for transfers between devices: 11 us -> 7.53 us
  starting transfers between devices: 56.2 us -> 52.8 us
  local copies, waits for them, and re-layouts: 6.53 us -> 5.17 us
    all_to_all x1, waiting for transfers between devices: 10.9 us -> 7.5 us  [shards(): met = lax.all_to_all(pieces, ('dp', 'ctx'), 0, 0, tiled=True)]
    another operation x1 -> x0, local copies, waits for them, and re-layouts: 2.92 us -> none  [owner_sums(): pieces = partial_value.reshape(groups, members, own).transpose(1, 0, 2)]
    all_to_all x1, starting transfers between devices: 26.9 us -> 24.3 us  [shards(): met = lax.all_to_all(pieces, ('dp', 'ctx'), 0, 0, tiled=True)]
    unnamed x15 -> x34, local copies, waits for them, and re-layouts: 2.12 us -> 4.49 us
    pallas_call x1, Pallas kernels: 2.17 us -> 0.32 us  [prepare(): pl.pallas_call(prepare_kernel, out_shape=(shape, shape), name='prepare',...]
    pallas_call x2 -> x3, Pallas kernels: 16.7 us -> 18.6 us  [the longest x1 9.04 us: convolve(): pl.pallas_call(lambda *refs: convolve_kernel(group_size, *refs), grid=(ch...]
    ppermute x10 -> x12, starting transfers between devices: 29.4 us -> 28.5 us  [the longest x6 16.2 us: swapped(): lax.ppermute(x, 'ctx', [(i, i ^ 1) for i in range(lax.axis_size('ctx'))])]
  transfers between devices with their start and end apart: 11 -> 13, of which waited for: 1 -> 1; matrix products, arithmetic and copies ran while one was open for 5% -> 0% of each run, Pallas kernels for 13% -> 26%
where the time goes in v2:
time: 91.1 us; the launch traced here: 90.3 us
  starting transfers between devices  52.8 us (58%)
  Pallas kernels  23.7 us (26%)
  waiting for transfers between devices  7.53 us (8%)
  local copies, waits for them, and re-layouts  5.17 us (6%)
  between operations  0.99 us (1%)
    all_to_all x1, starting transfers between devices, shards(): met = lax.all_to_all(pieces, ('dp', 'ctx'), 0, 0, tiled=True)  24.3 us
    ppermute x6, starting transfers between devices, swapped(): lax.ppermute(x, 'ctx', [(i, i ^ 1) for i in range(lax.axis_size('ctx'))])  16.2 us
    ppermute x6, starting transfers between devices, moved(): return lax.ppermute(x, 'ctx', pairs)  12.3 us
    pallas_call x1, Pallas kernels, convolve(): pl.pallas_call(lambda *refs: convolve_kernel(group_size, *refs), grid=(ch...  9.04 us
    all_to_all x1, waiting for transfers between devices, shards(): met = lax.all_to_all(pieces, ('dp', 'ctx'), 0, 0, tiled=True)  7.5 us
    pallas_call x1, Pallas kernels, toeplitz(): pl.pallas_call(toeplitz_kernel, grid=(groups // step,), in_specs=[pl.Bloc...  4.77 us
    pallas_call x1, Pallas kernels, pair_sums(): pl.pallas_call(lambda *refs: far_kernel(group_size, *refs), grid=(chunks,...  4.76 us
    pallas_call x1, Pallas kernels, pair_sums(): pl.pallas_call(lambda *refs: near_kernel(group_size, *refs), grid=(chunks...  4.76 us
  transfers between devices with their start and end apart: 13, of which 1 were waited for; matrix products, arithmetic and copies ran while one was open for 0% of the time, Pallas kernels for 26%

profile of v2, /device:TPU:24, one launch (start us, length us, event | category | flops | bytes accessed | tf_op | source)
XLA Modules:
  0.0 90.3 jit_solution(14156790110883986265)
XLA Ops:
  0.6 0.9 %copy-done = bf16[1,128,1024]{2,1,0:T(8,128)(2,1)S(1)} copy-done((bf16[1,128,1024]{2,1,0:T(8,128)(2,1)S(1)}, bf16[1,128,1024]{2,1,0:T(8,128)(2,1)}, u32[]{:S(2)}) %copy-start) | copy-done | bytes 262168
  1.6 0.9 %copy-done.1 = bf16[1,128,1024]{2,1,0:T(8,128)(2,1)S(1)} copy-done((bf16[1,128,1024]{2,1,0:T(8,128)(2,1)S(1)}, bf16[1,128,1024]{2,1,0:T(8,128)(2,1)}, u32[]{:S(2)}) %copy-start.1) | copy-done | bytes 262168
  2.5 0.9 %copy-done.2 = bf16[1,128,1024]{2,1,0:T(8,128)(2,1)S(1)} copy-done((bf16[1,128,1024]{2,1,0:T(8,128)(2,1)S(1)}, bf16[1,128,1024]{2,1,0:T(8,128)(2,1)}, u32[]{:S(2)}) %copy-start.2) | copy-done | bytes 262168
  3.5 0.3 prepare.1
  3.8 1.3 %collective-permute-start.7 = (bf16[128,1024]{1,0:T(8,128)(2,1)S(1)}, bf16[128,1024]{1,0:T(8,128)(2,1)S(1)}, u32[]{:S(2)}, u32[]{:S(2)}) collective-permute-start(bf16[128,1024]{1,0:T(8,128)(2,1)S(1)} %get-tuple-element.10.refs_11_.refs_1_), channel_id=1, source_target_pairs={{8,0},{12,4},{16,8},{20,12},{24,16},{28,20},{32,24},{36,28},{40,32... | collective-permute-start | bytes 786440 | tf_op jit(solution)/shard_map/ppermute | solution.py:274
  5.1 1.9 %collective-permute-start.6 = (bf16[128,1024]{1,0:T(8,128)(2,1)S(1)}, bf16[128,1024]{1,0:T(8,128)(2,1)S(1)}, u32[]{:S(2)}, u32[]{:S(2)}) collective-permute-start(bf16[128,1024]{1,0:T(8,128)(2,1)S(1)} %get-tuple-element.10.refs_11_.refs_1_), channel_id=1, source_target_pairs={{0,4},{4,0},{8,12},{12,8},{16,20},{20,16},{24,28},{28,24},{32,36},... | collective-permute-start | bytes 786440 | tf_op jit(solution)/shard_map/ppermute | solution.py:278
  7.1 4.6 %collective-permute-start.1 = (bf16[128,1024]{1,0:T(8,128)(2,1)S(1)}, bf16[128,1024]{1,0:T(8,128)(2,1)S(1)}, u32[]{:S(2)}, u32[]{:S(2)}) collective-permute-start(bf16[128,1024]{1,0:T(8,128)(2,1)S(1)} %get-tuple-element.9.refs_4_), channel_id=1, source_target_pairs={{0,8},{4,12},{8,16},{12,20},{16,24},{20,28},{24,32},{28,36},{32,40... | collective-permute-start | bytes 786440 | tf_op jit(solution)/shard_map/ppermute | solution.py:274
  11.6 2.1 %collective-permute-start = (bf16[128,1024]{1,0:T(8,128)(2,1)S(1)}, bf16[128,1024]{1,0:T(8,128)(2,1)S(1)}, u32[]{:S(2)}, u32[]{:S(2)}) collective-permute-start(bf16[128,1024]{1,0:T(8,128)(2,1)S(1)} %get-tuple-element.9.refs_4_), channel_id=1, source_target_pairs={{0,4},{4,0},{8,12},{12,8},{16,20},{20,16},{24,28},{28,24},{32,36},... | collective-permute-start | bytes 786440 | tf_op jit(solution)/shard_map/ppermute | solution.py:278
  13.8 4.8 %toeplitz.1.refs_1_ = bf16[32,128,768]{2,1,0:T(8,128)(2,1)} custom-call(bf16[32,640]{1,0:T(8,128)(2,1)} %taps_ref.1), custom_call_target="tpu_custom_call" | custom-call | flops 12000000000 | bytes 6400000 | tf_op jit(solution)/shard_map/toeplitz/pallas_call | solution.py:57
  18.5 0.0 collective-permute-done.1.refs_6_.refs_5_.refs_4_
  18.5 3.8 %collective-permute-start.3 = (bf16[128,1024]{1,0:T(8,128)(2,1)S(1)}, bf16[128,1024]{1,0:T(8,128)(2,1)S(1)}, u32[]{:S(2)}, u32[]{:S(2)}) collective-permute-start(bf16[128,1024]{1,0:T(8,128)(2,1)S(1)} %collective-permute-done.1.refs_6_.refs_5_.refs_4_), channel_id=1, source_target_pairs={{0,8},{4,12},{8,16},{12,20},{16,24},{20,28},{24,32},{28,36},{32,40... | collective-permute-start | bytes 786440 | tf_op jit(solution)/shard_map/ppermute | solution.py:274
  22.4 1.9 %collective-permute-start.2 = (bf16[128,1024]{1,0:T(8,128)(2,1)S(1)}, bf16[128,1024]{1,0:T(8,128)(2,1)S(1)}, u32[]{:S(2)}, u32[]{:S(2)}) collective-permute-start(bf16[128,1024]{1,0:T(8,128)(2,1)S(1)} %collective-permute-done.1.refs_6_.refs_5_.refs_4_), channel_id=1, source_target_pairs={{0,4},{4,0},{8,12},{12,8},{16,20},{20,16},{24,28},{28,24},{32,36},... | collective-permute-start | bytes 786440 | tf_op jit(solution)/shard_map/ppermute | solution.py:278
  24.3 0.0 collective-permute-done.7.refs_13_.refs_3_
  24.3 1.3 %collective-permute-start.9 = (bf16[128,1024]{1,0:T(8,128)(2,1)S(1)}, bf16[128,1024]{1,0:T(8,128)(2,1)S(1)}, u32[]{:S(2)}, u32[]{:S(2)}) collective-permute-start(bf16[128,1024]{1,0:T(8,128)(2,1)S(1)} %collective-permute-done.7.refs_13_.refs_3_), channel_id=1, source_target_pairs={{8,0},{12,4},{16,8},{20,12},{24,16},{28,20},{32,24},{36,28},{40,32... | collective-permute-start | bytes 786440 | tf_op jit(solution)/shard_map/ppermute | solution.py:274
  25.6 2.4 %collective-permute-start.8 = (bf16[128,1024]{1,0:T(8,128)(2,1)S(1)}, bf16[128,1024]{1,0:T(8,128)(2,1)S(1)}, u32[]{:S(2)}, u32[]{:S(2)}) collective-permute-start(bf16[128,1024]{1,0:T(8,128)(2,1)S(1)} %collective-permute-done.7.refs_13_.refs_3_), channel_id=1, source_target_pairs={{0,4},{4,0},{8,12},{12,8},{16,20},{20,16},{24,28},{28,24},{32,36},... | collective-permute-start | bytes 786440 | tf_op jit(solution)/shard_map/ppermute | solution.py:278
  28.1 4.8 %pair_near.1.refs_1_ = f32[8,4,640]{2,1,0:T(4,128)S(1)} custom-call(s32[1]{0:T(128)} %bitcast.refs_0_, bf16[128,1024]{1,0:T(8,128)(2,1)S(1)} %get-tuple-element.10.refs_11_.refs_1_, bf16[128,1024]{1,0:T(8,128)(2,1)S(1)} %collective-permute-done.6.refs_12_.refs_2_, bf16[128,1024]{1,0:T(8,128)(2,1)S(1)} %collective-permute-done.7.refs_13_.refs_3_, ...), custom_call_target="tpu_custom_call" | custom-call | flops 8000000000 | bytes 1500000 | tf_op jit(solution)/shard_map/pair_near/pallas_call | solution.py:176
  32.9 1.9 %collective-permute-start.4 = (bf16[128,1024]{1,0:T(8,128)(2,1)S(1)}, bf16[128,1024]{1,0:T(8,128)(2,1)S(1)}, u32[]{:S(2)}, u32[]{:S(2)}) collective-permute-start(bf16[128,1024]{1,0:T(8,128)(2,1)S(1)} %collective-permute-done.3.refs_8_.refs_5_), channel_id=1, source_target_pairs={{0,4},{4,0},{8,12},{12,8},{16,20},{20,16},{24,28},{28,24},{32,36},... | collective-permute-start | bytes 786440 | tf_op jit(solution)/shard_map/ppermute | solution.py:278
  34.8 0.0 collective-permute-done.refs_5_
  34.8 0.7 collective-permute-start.5
  35.5 5.9 %collective-permute-start.10 = (bf16[128,1024]{1,0:T(8,128)(2,1)S(1)}, bf16[128,1024]{1,0:T(8,128)(2,1)S(1)}, u32[]{:S(2)}, u32[]{:S(2)}) collective-permute-start(bf16[128,1024]{1,0:T(8,128)(2,1)S(1)} %collective-permute-done.9.refs_15_), channel_id=1, source_target_pairs={{0,4},{4,0},{8,12},{12,8},{16,20},{20,16},{24,28},{28,24},{32,36},... | collective-permute-start | bytes 786440 | tf_op jit(solution)/shard_map/ppermute | solution.py:278
  41.5 0.7 collective-permute-start.11
  42.2 4.8 %pair_far.1 = f32[128,1,160]{2,1,0:T(1,128)} custom-call(s32[1]{0:T(128)} %bitcast.refs_0_, f32[8,4,640]{2,1,0:T(4,128)S(1)} %pair_near.1.refs_1_, bf16[128,1024]{1,0:T(8,128)(2,1)S(1)} %collective-permute-done.6.refs_12_.refs_2_, bf16[128,1024]{1,0:T(8,128)(2,1)S(1)} %collective-permute-done.8.refs_14_.refs_3_, ...), custom_call_target="tpu_custom_call" | custom-call | flops 4000000000 | bytes 1500000 | tf_op jit(solution)/shard_map/pair_far/pallas_call | solution.py:186
  46.9 24.3 %all-to-all-start = ((f32[128,1,160]{2,1,0:T(1,128)}), f32[128,1,160]{2,1,0:T(1,128)S(1)}, u32[]{:S(2)}, u32[]{:S(2)}) async-start(f32[128,1,160]{2,1,0:T(1,128)} %pair_far.1), calls=%async_computation | async-start | bytes 262144 | tf_op jit(solution)/shard_map/all_to_all | solution.py:311
  71.3 0.7 copy-done.11
  71.9 0.1 copy-done.13
  72.0 0.1 copy-done.14
  72.1 0.1 copy-done.15
  72.2 0.7 copy-done.16
  72.9 9.0 %convolve.1 = (bf16[128,1024]{1,0:T(8,128)(2,1)}, bf16[128,1024]{1,0:T(8,128)(2,1)}, bf16[128,1024]{1,0:T(8,128)(2,1)}) custom-call(s32[1]{0:T(128)} %bitcast.refs_0_, bf16[32,128,768]{2,1,0:T(8,128)(2,1)} %toeplitz.1.refs_1_, bf16[128,1024]{1,0:T(8,128)(2,1)} %bitcast.9, bf16[128,1024]{1,0:T(8,128)(2,1)} %bitcast.11, bf16[128,1024]{1,0:T(8,128)(2,1)} %copy-done.4, ...), custom_call_target="tpu_custom_call" | custom-call | flops 12000000000 | bytes 10500000 | tf_op jit(solution)/shard_map/convolve/pallas_call | solution.py:251
  81.9 7.5 %all-to-all-done = f32[128,1,160]{2,1,0:T(1,128)S(1)} async-done(((f32[128,1,160]{2,1,0:T(1,128)}), f32[128,1,160]{2,1,0:T(1,128)S(1)}, u32[]{:S(2)}, u32[]{:S(2)}) %all-to-all-start) | async-done | bytes 81952 | tf_op jit(solution)/shard_map/all_to_all | solution.py:311
  89.4 0.2 reduce_sum.9
  89.6 0.7 div.12
  (36 shorter events, 0.1 us)
Async XLA Ops:
  0.6 1.0 %copy-start = (bf16[1,128,1024]{2,1,0:T(8,128)(2,1)S(1)}, bf16[1,128,1024]{2,1,0:T(8,128)(2,1)}, u32[]{:S(2)}) copy-start(bf16[1,128,1024]{2,1,0:T(8,128)(2,1)} %param.5) | copy-start | bytes 786436
  1.6 0.9 %copy-start.1 = (bf16[1,128,1024]{2,1,0:T(8,128)(2,1)S(1)}, bf16[1,128,1024]{2,1,0:T(8,128)(2,1)}, u32[]{:S(2)}) copy-start(bf16[1,128,1024]{2,1,0:T(8,128)(2,1)} %param.4) | copy-start | bytes 786436
  2.5 0.9 %copy-start.2 = (bf16[1,128,1024]{2,1,0:T(8,128)(2,1)S(1)}, bf16[1,128,1024]{2,1,0:T(8,128)(2,1)}, u32[]{:S(2)}) copy-start(bf16[1,128,1024]{2,1,0:T(8,128)(2,1)} %param.6) | copy-start | bytes 786436
  3.8 24.2 %copy-start.3 = (bf16[128,1024]{1,0:T(8,128)(2,1)}, bf16[128,1024]{1,0:T(8,128)(2,1)S(1)}, u32[]{:S(2)}) copy-start(bf16[128,1024]{1,0:T(8,128)(2,1)S(1)} %get-tuple-element.10.refs_11_.refs_1_) | copy-start | bytes 786436
  3.8 24.2 %copy-start.4 = (bf16[128,1024]{1,0:T(8,128)(2,1)}, bf16[128,1024]{1,0:T(8,128)(2,1)S(1)}, u32[]{:S(2)}) copy-start(bf16[128,1024]{1,0:T(8,128)(2,1)S(1)} %get-tuple-element.9.refs_4_) | copy-start | bytes 786436
  3.8 20.5 %collective-permute-start.7 = (bf16[128,1024]{1,0:T(8,128)(2,1)S(1)}, bf16[128,1024]{1,0:T(8,128)(2,1)S(1)}, u32[]{:S(2)}, u32[]{:S(2)}) collective-permute-start(bf16[128,1024]{1,0:T(8,128)(2,1)S(1)} %get-tuple-element.10.refs_11_.refs_1_), channel_id=1, source_target_pairs={{8,0},{12,4},{16,8},{20,12},{24,16},{28,20},{32,24},{36,28},{40,32... | collective-permute-start | bytes 786440 | tf_op jit(solution)/shard_map/ppermute | solution.py:274
  5.1 20.5 %collective-permute-start.6 = (bf16[128,1024]{1,0:T(8,128)(2,1)S(1)}, bf16[128,1024]{1,0:T(8,128)(2,1)S(1)}, u32[]{:S(2)}, u32[]{:S(2)}) collective-permute-start(bf16[128,1024]{1,0:T(8,128)(2,1)S(1)} %get-tuple-element.10.refs_11_.refs_1_), channel_id=1, source_target_pairs={{0,4},{4,0},{8,12},{12,8},{16,20},{20,16},{24,28},{28,24},{32,36},... | collective-permute-start | bytes 786440 | tf_op jit(solution)/shard_map/ppermute | solution.py:278
  7.1 11.5 %collective-permute-start.1 = (bf16[128,1024]{1,0:T(8,128)(2,1)S(1)}, bf16[128,1024]{1,0:T(8,128)(2,1)S(1)}, u32[]{:S(2)}, u32[]{:S(2)}) collective-permute-start(bf16[128,1024]{1,0:T(8,128)(2,1)S(1)} %get-tuple-element.9.refs_4_), channel_id=1, source_target_pairs={{0,8},{4,12},{8,16},{12,20},{16,24},{20,28},{24,32},{28,36},{32,40... | collective-permute-start | bytes 786440 | tf_op jit(solution)/shard_map/ppermute | solution.py:274
  11.6 23.2 %collective-permute-start = (bf16[128,1024]{1,0:T(8,128)(2,1)S(1)}, bf16[128,1024]{1,0:T(8,128)(2,1)S(1)}, u32[]{:S(2)}, u32[]{:S(2)}) collective-permute-start(bf16[128,1024]{1,0:T(8,128)(2,1)S(1)} %get-tuple-element.9.refs_4_), channel_id=1, source_target_pairs={{0,4},{4,0},{8,12},{12,8},{16,20},{20,16},{24,28},{28,24},{32,36},... | collective-permute-start | bytes 786440 | tf_op jit(solution)/shard_map/ppermute | solution.py:278
  18.5 23.6 %copy-start.7 = (bf16[128,1024]{1,0:T(8,128)(2,1)}, bf16[128,1024]{1,0:T(8,128)(2,1)S(1)}, u32[]{:S(2)}) copy-start(bf16[128,1024]{1,0:T(8,128)(2,1)S(1)} %collective-permute-done.1.refs_6_.refs_5_.refs_4_) | copy-start | bytes 786436
  18.5 14.3 %collective-permute-start.3 = (bf16[128,1024]{1,0:T(8,128)(2,1)S(1)}, bf16[128,1024]{1,0:T(8,128)(2,1)S(1)}, u32[]{:S(2)}, u32[]{:S(2)}) collective-permute-start(bf16[128,1024]{1,0:T(8,128)(2,1)S(1)} %collective-permute-done.1.refs_6_.refs_5_.refs_4_), channel_id=1, source_target_pairs={{0,8},{4,12},{8,16},{12,20},{16,24},{20,28},{24,32},{28,36},{32,40... | collective-permute-start | bytes 786440 | tf_op jit(solution)/shard_map/ppermute | solution.py:274
  22.4 48.8 %collective-permute-start.2 = (bf16[128,1024]{1,0:T(8,128)(2,1)S(1)}, bf16[128,1024]{1,0:T(8,128)(2,1)S(1)}, u32[]{:S(2)}, u32[]{:S(2)}) collective-permute-start(bf16[128,1024]{1,0:T(8,128)(2,1)S(1)} %collective-permute-done.1.refs_6_.refs_5_.refs_4_), channel_id=1, source_target_pairs={{0,4},{4,0},{8,12},{12,8},{16,20},{20,16},{24,28},{28,24},{32,36},... | collective-permute-start | bytes 786440 | tf_op jit(solution)/shard_map/ppermute | solution.py:278
  24.3 8.5 %copy-start.5 = (bf16[128,1024]{1,0:T(8,128)(2,1)}, bf16[128,1024]{1,0:T(8,128)(2,1)S(1)}, u32[]{:S(2)}) copy-start(bf16[128,1024]{1,0:T(8,128)(2,1)S(1)} %collective-permute-done.7.refs_13_.refs_3_) | copy-start | bytes 786436
  24.3 11.2 %collective-permute-start.9 = (bf16[128,1024]{1,0:T(8,128)(2,1)S(1)}, bf16[128,1024]{1,0:T(8,128)(2,1)S(1)}, u32[]{:S(2)}, u32[]{:S(2)}) collective-permute-start(bf16[128,1024]{1,0:T(8,128)(2,1)S(1)} %collective-permute-done.7.refs_13_.refs_3_), channel_id=1, source_target_pairs={{8,0},{12,4},{16,8},{20,12},{24,16},{28,20},{32,24},{36,28},{40,32... | collective-permute-start | bytes 786440 | tf_op jit(solution)/shard_map/ppermute | solution.py:274
  25.6 16.5 %copy-start.6 = (bf16[128,1024]{1,0:T(8,128)(2,1)}, bf16[128,1024]{1,0:T(8,128)(2,1)S(1)}, u32[]{:S(2)}) copy-start(bf16[128,1024]{1,0:T(8,128)(2,1)S(1)} %collective-permute-done.6.refs_12_.refs_2_) | copy-start | bytes 786436
  25.6 15.8 %collective-permute-start.8 = (bf16[128,1024]{1,0:T(8,128)(2,1)S(1)}, bf16[128,1024]{1,0:T(8,128)(2,1)S(1)}, u32[]{:S(2)}, u32[]{:S(2)}) collective-permute-start(bf16[128,1024]{1,0:T(8,128)(2,1)S(1)} %collective-permute-done.7.refs_13_.refs_3_), channel_id=1, source_target_pairs={{0,4},{4,0},{8,12},{12,8},{16,20},{20,16},{24,28},{28,24},{32,36},... | collective-permute-start | bytes 786440 | tf_op jit(solution)/shard_map/ppermute | solution.py:278
  32.9 14.1 %copy-start.8 = (bf16[128,1024]{1,0:T(8,128)(2,1)}, bf16[128,1024]{1,0:T(8,128)(2,1)S(1)}, u32[]{:S(2)}) copy-start(bf16[128,1024]{1,0:T(8,128)(2,1)S(1)} %collective-permute-done.3.refs_8_.refs_5_) | copy-start | bytes 786436
  32.9 38.4 %collective-permute-start.4 = (bf16[128,1024]{1,0:T(8,128)(2,1)S(1)}, bf16[128,1024]{1,0:T(8,128)(2,1)S(1)}, u32[]{:S(2)}, u32[]{:S(2)}) collective-permute-start(bf16[128,1024]{1,0:T(8,128)(2,1)S(1)} %collective-permute-done.3.refs_8_.refs_5_), channel_id=1, source_target_pairs={{0,4},{4,0},{8,12},{12,8},{16,20},{20,16},{24,28},{28,24},{32,36},... | collective-permute-start | bytes 786440 | tf_op jit(solution)/shard_map/ppermute | solution.py:278
  34.8 12.1 %copy-start.10 = (bf16[128,1024]{1,0:T(8,128)(2,1)}, bf16[128,1024]{1,0:T(8,128)(2,1)S(1)}, u32[]{:S(2)}) copy-start(bf16[128,1024]{1,0:T(8,128)(2,1)S(1)} %collective-permute-done.refs_5_) | copy-start | bytes 786436
  34.8 36.4 %collective-permute-start.5 = (bf16[128,1024]{1,0:T(8,128)(2,1)S(1)}, bf16[128,1024]{1,0:T(8,128)(2,1)S(1)}, u32[]{:S(2)}, u32[]{:S(2)}) collective-permute-start(bf16[128,1024]{1,0:T(8,128)(2,1)S(1)} %collective-permute-done.3.refs_8_.refs_5_), channel_id=1, source_target_pairs={{4,8},{12,16},{20,24},{28,32},{36,40},{44,48},{52,56},{60,64},{68,... | collective-permute-start | bytes 786440 | tf_op jit(solution)/shard_map/ppermute | solution.py:274
  35.5 11.4 %copy-start.12 = (bf16[128,1024]{1,0:T(8,128)(2,1)}, bf16[128,1024]{1,0:T(8,128)(2,1)S(1)}, u32[]{:S(2)}) copy-start(bf16[128,1024]{1,0:T(8,128)(2,1)S(1)} %collective-permute-done.9.refs_15_) | copy-start | bytes 786436
  35.5 35.7 %collective-permute-start.10 = (bf16[128,1024]{1,0:T(8,128)(2,1)S(1)}, bf16[128,1024]{1,0:T(8,128)(2,1)S(1)}, u32[]{:S(2)}, u32[]{:S(2)}) collective-permute-start(bf16[128,1024]{1,0:T(8,128)(2,1)S(1)} %collective-permute-done.9.refs_15_), channel_id=1, source_target_pairs={{0,4},{4,0},{8,12},{12,8},{16,20},{20,16},{24,28},{28,24},{32,36},... | collective-permute-start | bytes 786440 | tf_op jit(solution)/shard_map/ppermute | solution.py:278
  41.4 5.5 %copy-start.9 = (bf16[128,1024]{1,0:T(8,128)(2,1)}, bf16[128,1024]{1,0:T(8,128)(2,1)S(1)}, u32[]{:S(2)}) copy-start(bf16[128,1024]{1,0:T(8,128)(2,1)S(1)} %collective-permute-done.8.refs_14_.refs_3_) | copy-start | bytes 786436
  41.5 29.8 %collective-permute-start.11 = (bf16[128,1024]{1,0:T(8,128)(2,1)S(1)}, bf16[128,1024]{1,0:T(8,128)(2,1)S(1)}, u32[]{:S(2)}, u32[]{:S(2)}) collective-permute-start(bf16[128,1024]{1,0:T(8,128)(2,1)S(1)} %collective-permute-done.9.refs_15_), channel_id=1, source_target_pairs={{8,4},{16,12},{24,20},{32,28},{40,36},{48,44},{56,52},{64,60},{72,... | collective-permute-start | bytes 786440 | tf_op jit(solution)/shard_map/ppermute | solution.py:274
  46.9 42.5 %all-to-all-start = ((f32[128,1,160]{2,1,0:T(1,128)}), f32[128,1,160]{2,1,0:T(1,128)S(1)}, u32[]{:S(2)}, u32[]{:S(2)}) async-start(f32[128,1,160]{2,1,0:T(1,128)} %pair_far.1), calls=%async_computation | async-start | bytes 262144 | tf_op jit(solution)/shard_map/all_to_all | solution.py:311
  71.2 0.7 copy-start.11
  71.2 0.8 copy-start.13
  71.2 0.9 copy-start.14
  71.3 0.9 %copy-start.15 = (bf16[128,1024]{1,0:T(8,128)(2,1)}, bf16[128,1024]{1,0:T(8,128)(2,1)S(1)}, u32[]{:S(2)}) copy-start(bf16[128,1024]{1,0:T(8,128)(2,1)S(1)} %collective-permute-done.10.refs_16_) | copy-start | bytes 786436
  72.2 0.7 copy-start.16

commit v3 on v2

--- a/solution.py
+++ b/solution.py
@@ -9,6 +9,7 @@
 
 LANES = 128
 SCOPED = 16 * 1024 * 1024
+CROSS = jnp.float32
 
 
 def exchange_matrix(size):
@@ -35,33 +36,38 @@
         prepare_kernel,
         out_shape=(shape, shape),
         name="prepare",
-        compiler_params=pltpu.CompilerParams(vmem_limit_bytes=SCOPED),
         cost_estimate=pl.CostEstimate(flops=40_000_000, bytes_accessed=1_400_000, transcendentals=0),
     )(gate_rows, value_rows, grad_rows)
 
 
-def toeplitz_kernel(taps_ref, matrix_ref):
-    groups, tok_rows, width = matrix_ref.shape
+def toeplitz_kernel(taps_ref, even_ref, odd_ref):
+    groups, tok_rows, width = even_ref.shape
     taps = taps_ref[...].astype(jnp.float32)
-    padded = jnp.concatenate([taps, jnp.zeros((groups, width - taps.shape[1]), jnp.float32)], axis=1)
+    padded = jnp.concatenate(
+        [taps, jnp.zeros((groups, 2 * width - taps.shape[1]), jnp.float32)], axis=1
+    )
     for g in range(groups):
-        spread = jnp.broadcast_to(padded[g : g + 1, :], (tok_rows, width))
-        sheared = pltpu.roll(spread, 0, 1, stride=1, stride_axis=0)
-        matrix_ref[g] = sheared.astype(jnp.bfloat16)
+        spread = jnp.broadcast_to(padded[g : g + 1, :], (tok_rows, 2 * width))
+        sheared = pltpu.roll(spread, 0, 1, stride=1, stride_axis=0).astype(jnp.bfloat16)
+        for at in range(0, width, tok_rows):
+            even_ref[g, :, at : at + tok_rows] = sheared[:, 2 * at : 2 * at + tok_rows]
+            odd_ref[g, :, at : at + tok_rows] = sheared[:, 2 * at + tok_rows : 2 * at + 2 * tok_rows]
 
 
 def toeplitz(taps, tok_rows):
     groups, lag_count = taps.shape
     step = 8
-    width = lag_count + tok_rows
+    width = (lag_count + tok_rows) // 2
+    spec = pl.BlockSpec((step, tok_rows, width), lambda i: (i, 0, 0))
+    shape = jax.ShapeDtypeStruct((groups, tok_rows, width), jnp.bfloat16)
     return pl.pallas_call(
         toeplitz_kernel,
         grid=(groups // step,),
         in_specs=[pl.BlockSpec((step, lag_count), lambda i: (i, 0))],
-        out_specs=pl.BlockSpec((step, tok_rows, width), lambda i: (i, 0, 0)),
-        out_shape=jax.ShapeDtypeStruct((groups, tok_rows, width), jnp.bfloat16),
+        out_specs=[spec, spec],
+        out_shape=[shape, shape],
         name="toeplitz",
-        cost_estimate=pl.CostEstimate(flops=12_000_000_000, bytes_accessed=6_400_000, transcendentals=0),
+        cost_estimate=pl.CostEstimate(flops=8_000_000_000, bytes_accessed=6_400_000, transcendentals=0),
     )(taps)
 
 
@@ -123,7 +129,7 @@
 
 
 def far_kernel(
-    group_size, parity_ref, near_ref, mixed_swap, mixed_swap_one, value_one, value_two, out_ref, held_ref
+    group_size, parity_ref, near_ref, mixed_swap, value_one, value_two, value_three, out_ref, held_ref, turned_ref
 ):
     step = pl.program_id(0)
     tok_rows = mixed_swap.shape[0]
@@ -131,10 +137,10 @@
     owner = lane_group((tok_rows, LANES), group_size)
     parity = parity_ref[0]
     third = parity_select(parity, value_one[...], value_two[...])
-    fifth = parity_select(parity, mixed_swap[...], mixed_swap_one[...])
+    fifth = parity_select(parity, value_two[...], value_three[...])
     windows = {
         3: lag_window(mixed_swap[...], third, owner, per_chunk),
-        5: lag_window(fifth, value_two[...], owner, per_chunk),
+        5: lag_window(mixed_swap[...], fifth, owner, per_chunk),
     }
     held_ref[step] = near_ref[0] + gathered_windows(
         windows, lag_count // tok_rows, per_chunk, tok_rows
@@ -146,21 +152,12 @@
         members = out_ref.shape[0]
         own = lag_count // members
         sums = jnp.concatenate([held_ref[i] for i in range(chunks)], axis=0)
-        high = sums.astype(jnp.bfloat16)
-        rest = sums - high.astype(jnp.float32)
-        middle = rest.astype(jnp.bfloat16)
-        low = (rest - middle.astype(jnp.float32)).astype(jnp.bfloat16)
-        lags = lax.broadcasted_iota(jnp.int32, (lag_count, lag_count), 0)
-        cols = lax.broadcasted_iota(jnp.int32, (lag_count, lag_count), 1)
-        picks = jnp.where(lags == own * (cols % members) + cols // members, 1.0, 0.0)
-        split = jnp.dot(
-            jnp.concatenate([high, middle, low], axis=0),
-            picks.astype(jnp.bfloat16),
-            preferred_element_type=jnp.float32,
-        )
-        moved = split[:groups] + split[groups : 2 * groups] + split[2 * groups :]
+        filler = jnp.zeros((LANES - groups, LANES), jnp.float32)
+        for at in range(0, lag_count, LANES):
+            square = jnp.concatenate([sums[:, at : at + LANES], filler], axis=0)
+            turned_ref[at : at + LANES, :] = square.T
         out_ref[:, 0, :] = jnp.concatenate(
-            [moved[:, r * members : (r + 1) * members].T for r in range(own)], axis=1
+            [turned_ref[pl.ds(r, members, stride=own), :][:, :groups] for r in range(own)], axis=1
         )
 
 
@@ -189,40 +186,18 @@
         in_specs=[scalar, part] + [spec] * 4,
         out_specs=pl.BlockSpec((members, 1, groups * own), lambda i: (0, 0, 0)),
         out_shape=jax.ShapeDtypeStruct((members, 1, groups * own), jnp.float32),
-        scratch_shapes=[pltpu.VMEM((chunks, per_chunk, lag_count), jnp.float32)],
+        scratch_shapes=[
+            pltpu.VMEM((chunks, per_chunk, lag_count), jnp.float32),
+            pltpu.VMEM((lag_count, LANES), jnp.float32),
+        ],
         name="pair_far",
         compiler_params=pltpu.CompilerParams(vmem_limit_bytes=SCOPED),
         cost_estimate=pl.CostEstimate(flops=4_000_000_000, bytes_accessed=1_500_000, transcendentals=0),
-    )(parity, near, mixed["swap"], mixed["swap_one"], values["one"], values["two"])
-
-
-NAMES = ("own", "swap", "one", "swap_one", "two", "swap_two", "three")
-
-
-def convolve_kernel(group_size, *refs):
-    parity_ref, matrix_ref, gate_ref, grad_ref = refs[:4]
-    value = {name: ref[...] for name, ref in zip(NAMES, refs[4:11])}
-    mixed = {name: ref[...] for name, ref in zip(NAMES, refs[11:18])}
-    output_ref, grad_gate_ref, grad_conv_ref = refs[18:]
+    )(parity, near, mixed["swap"], values["one"], values["two"], values["three"])
+
+
+def group_product(matrix_ref, values, mixes, group_size):
     per_chunk, tok_rows, width = matrix_ref.shape
-    parity = parity_ref[0]
-    flip = exchange_matrix(tok_rows)
-    values = [
-        value["own"],
-        parity_select(parity, value["swap_one"], value["swap"]),
-        value["one"],
-        parity_select(parity, value["swap_two"], value["swap_one"]),
-        value["two"],
-        parity_select(parity, value["three"], value["swap_two"]),
-    ]
-    mixes = [
-        mixed["own"],
-        parity_select(parity, mixed["swap"], mixed["swap_one"]),
-        mixed["one"],
-        parity_select(parity, mixed["swap_one"], mixed["swap_two"]),
-        mixed["two"],
-        parity_select(parity, mixed["swap_two"], mixed["three"]),
-    ]
     right = jnp.concatenate(
         [jnp.concatenate([v, m], axis=1) for v, m in zip(values, mixes)], axis=0
     )
@@ -232,40 +207,72 @@
     chosen = product[:tok_rows]
     for g in range(1, per_chunk):
         chosen = jnp.where(owner == g, product[g * tok_rows : (g + 1) * tok_rows], chosen)
-    convolved = chosen[:, :LANES]
+    return chosen[:, :LANES], chosen[:, LANES:]
+
+
+def own_kernel(group_size, *refs):
+    matrix_ref = refs[0]
+    convolved, grads = group_product(
+        matrix_ref, [r[...] for r in refs[1:4]], [r[...] for r in refs[4:7]], group_size
+    )
+    out_ref = refs[7]
+    out_ref[0], out_ref[1] = convolved, grads
+
+
+def cross_kernel(group_size, *refs):
+    parity = refs[0][0]
+    value, mixed = [r[...] for r in refs[2:6]], [r[...] for r in refs[6:10]]
+    values = [parity_select(parity, value[m], value[m + 1]) for m in range(3)]
+    mixes = [parity_select(parity, mixed[m + 1], mixed[m]) for m in range(3)]
+    convolved, grads = group_product(refs[1], values, mixes, group_size)
+    out_ref = refs[10]
+    out_ref[0], out_ref[1] = convolved.astype(out_ref.dtype), grads.astype(out_ref.dtype)
+
+
+def finish_kernel(gate_ref, grad_ref, own_ref, met_ref, output_ref, grad_gate_ref, grad_conv_ref):
+    flip = exchange_matrix(gate_ref.shape[0])
+    convolved = own_ref[0] + met_ref[0].astype(jnp.float32)
     gate = jnp.dot(flip, gate_ref[...], preferred_element_type=jnp.float32)
     grad = jnp.dot(flip, grad_ref[...], preferred_element_type=jnp.float32)
     output_ref[...] = reversed_rows(flip, (gate * convolved).astype(jnp.bfloat16))
     grad_gate_ref[...] = reversed_rows(flip, (grad * convolved).astype(jnp.bfloat16))
-    grad_conv_ref[...] = chosen[:, LANES:].astype(jnp.bfloat16)
-
-
-def convolve(parity, matrix, gate_rows, grad_rows, values, mixed, group_size):
+    grad_conv_ref[...] = (own_ref[1] + met_ref[1].astype(jnp.float32)).astype(jnp.bfloat16)
+
+
+def half_convolve(kernel, name, matrix, blocks, group_size, kind, grant, leading=()):
     groups, tok_rows, width = matrix.shape
-    channels = gate_rows.shape[1]
-    chunks = channels // LANES
+    channels = blocks[0].shape[1]
     per_chunk = LANES // group_size
     spec = pl.BlockSpec((tok_rows, LANES), lambda i: (0, i))
-    scalar = pl.BlockSpec(memory_space=pltpu.SMEM)
+    return pl.pallas_call(
+        lambda *refs: kernel(group_size, *refs),
+        grid=(channels // LANES,),
+        in_specs=[pl.BlockSpec(memory_space=pltpu.SMEM)] * len(leading)
+        + [pl.BlockSpec((per_chunk, tok_rows, width), lambda i: (i, 0, 0))]
+        + [spec] * len(blocks),
+        out_specs=pl.BlockSpec((2, tok_rows, LANES), lambda i: (0, 0, i)),
+        out_shape=jax.ShapeDtypeStruct((2, tok_rows, channels), kind),
+        name=name,
+        compiler_params=pltpu.CompilerParams(vmem_limit_bytes=grant),
+        cost_estimate=pl.CostEstimate(flops=5_000_000_000, bytes_accessed=5_500_000, transcendentals=0),
+    )(*leading, matrix, *blocks)
+
+
+def finish(gate_rows, grad_rows, own_part, met_part):
+    tok_rows, channels = gate_rows.shape
+    lanes = 2 * LANES
+    spec = pl.BlockSpec((tok_rows, lanes), lambda i: (0, i))
+    pair = pl.BlockSpec((2, tok_rows, lanes), lambda i: (0, 0, i))
     shape = jax.ShapeDtypeStruct((tok_rows, channels), jnp.bfloat16)
     return pl.pallas_call(
-        lambda *refs: convolve_kernel(group_size, *refs),
-        grid=(chunks,),
-        in_specs=[scalar, pl.BlockSpec((per_chunk, tok_rows, width), lambda i: (i, 0, 0))]
-        + [spec] * 16,
+        finish_kernel,
+        grid=(channels // lanes,),
+        in_specs=[spec, spec, pair, pair],
         out_specs=[spec] * 3,
         out_shape=[shape] * 3,
-        name="convolve",
-        compiler_params=pltpu.CompilerParams(vmem_limit_bytes=59 * 1024 * 1024),
-        cost_estimate=pl.CostEstimate(flops=12_000_000_000, bytes_accessed=10_500_000, transcendentals=0),
-    )(
-        parity,
-        matrix,
-        gate_rows,
-        grad_rows,
-        *[values[name] for name in NAMES],
-        *[mixed[name] for name in NAMES],
-    )
+        name="finish",
+        cost_estimate=pl.CostEstimate(flops=200_000_000, bytes_accessed=3_500_000, transcendentals=0),
+    )(gate_rows, grad_rows, own_part, met_part)
 
 
 def moved(x, by, lands):
@@ -297,21 +304,20 @@
     values["one"] = moved(values["own"], 2, anyone)
     mixed["one"] = moved(mixed["own"], -2, anyone)
     mixed["swap"] = swapped(mixed["own"])
-    values["swap"] = swapped(values["own"])
-    matrix = toeplitz(kernel, tok_rows)
+    even_matrix, odd_matrix = toeplitz(kernel, tok_rows)
     values["two"] = moved(values["one"], 2, anyone)
     mixed["two"] = moved(mixed["one"], -2, anyone)
-    mixed["swap_one"] = swapped(mixed["one"])
-    values["swap_one"] = swapped(values["one"])
+    values["three"] = moved(values["two"], 2, odd)
+    mixed["three"] = moved(mixed["two"], -2, even)
     pieces = pair_sums(parity, mixed, values, group_size, lag_count, members)
-    values["three"] = moved(values["two"], 1, even)
-    mixed["three"] = moved(mixed["two"], -1, odd)
-    values["swap_two"] = swapped(values["two"])
-    mixed["swap_two"] = swapped(mixed["two"])
     met = lax.all_to_all(pieces, ("dp", "ctx"), 0, 0, tiled=True)
-    output, grad_gate, grad_conv = convolve(
-        parity, matrix, gate_rows, grad_rows, values, mixed, group_size
-    )
+    near = [t[name] for t in (values, mixed) for name in ("own", "one", "two")]
+    every = [t[name] for t in (values, mixed) for name in ("own", "one", "two", "three")]
+    own_part = half_convolve(own_kernel, "convolve_own", even_matrix, near, group_size, jnp.float32, None)
+    cross_part = half_convolve(
+        cross_kernel, "convolve_cross", odd_matrix, every, group_size, CROSS, SCOPED, (parity,)
+    )
+    output, grad_gate, grad_conv = finish(gate_rows, grad_rows, own_part, swapped(cross_part))
     summed = jnp.sum(met, axis=(0, 1)).reshape(lag_count // members, groups).T
     grad_kernel = summed / math.sqrt(lax.axis_size("dp") * tok_rows * blocks)
     return (output[None], grad_gate[None], grad_conv[None], grad_kernel)

time: 91.1 us -> 89.9 us (0.987)
  starting transfers between devices: 52.8 us -> 37.2 us
  waiting for transfers between devices: 7.53 us -> 19.6 us
  Pallas kernels: 23.7 us -> 30.8 us
  local copies, waits for them, and re-layouts: 5.17 us -> 0.7 us
    ppermute x6 -> x2, starting transfers between devices: 16.2 us -> 3.84 us  [swapped(): lax.ppermute(x, 'ctx', [(i, i ^ 1) for i in range(lax.axis_size('ctx'))])]
    ppermute x6, waiting for transfers between devices: 0.02 us -> 8.37 us  [moved(): return lax.ppermute(x, 'ctx', pairs)]
    pallas_call x1 -> x3, Pallas kernels: 9.04 us -> 14.6 us  [the longest x2 10.3 us: half_convolve(): pl.pallas_call(lambda *refs: kernel(group_size, *refs), grid=(channels //...]
    unnamed x34 -> x14, local copies, waits for them, and re-layouts: 4.49 us -> 0.03 us
    all_to_all x1, waiting for transfers between devices: 7.5 us -> 11.2 us  [shards(): met = lax.all_to_all(pieces, ('dp', 'ctx'), 0, 0, tiled=True)]
    all_to_all x1, starting transfers between devices: 24.3 us -> 20.6 us  [shards(): met = lax.all_to_all(pieces, ('dp', 'ctx'), 0, 0, tiled=True)]
    pallas_call x1, Pallas kernels: 0.32 us -> 2.16 us  [prepare(): pl.pallas_call(prepare_kernel, out_shape=(shape, shape), name='prepare',...]
  transfers between devices with their start and end apart: 13 -> 9, of which waited for: 1 -> 5; matrix products, arithmetic and copies ran while one was open for 0% -> 1% of each run, Pallas kernels for 26% -> 24%
where the time goes in v3:
time: 89.9 us; the launch traced here: 89.2 us
  starting transfers between devices  37.2 us (41%)
  Pallas kernels  30.8 us (34%)
  waiting for transfers between devices  19.6 us (22%)
    all_to_all x1, starting transfers between devices, shards(): met = lax.all_to_all(pieces, ('dp', 'ctx'), 0, 0, tiled=True)  20.6 us
    ppermute x6, starting transfers between devices, moved(): return lax.ppermute(x, 'ctx', pairs)  12.8 us
    all_to_all x1, waiting for transfers between devices, shards(): met = lax.all_to_all(pieces, ('dp', 'ctx'), 0, 0, tiled=True)  11.2 us
    pallas_call x2, Pallas kernels, half_convolve(): pl.pallas_call(lambda *refs: kernel(group_size, *refs), grid=(channels //...  10.3 us
    ppermute x6, waiting for transfers between devices, moved(): return lax.ppermute(x, 'ctx', pairs)  8.37 us
    pallas_call x1, Pallas kernels, pair_sums(): pl.pallas_call(lambda *refs: near_kernel(group_size, *refs), grid=(chunks...  4.76 us
    pallas_call x1, Pallas kernels, toeplitz(): pl.pallas_call(toeplitz_kernel, grid=(groups // step,), in_specs=[pl.Bloc...  4.69 us
    pallas_call x1, Pallas kernels, pair_sums(): pl.pallas_call(lambda *refs: far_kernel(group_size, *refs), grid=(chunks,...  4.59 us
  transfers between devices with their start and end apart: 9, of which 5 were waited for; matrix products, arithmetic and copies ran while one was open for 1% of the time, Pallas kernels for 24%

profile of v3, /device:TPU:24, one launch (start us, length us, event | category | flops | bytes accessed | tf_op | source)
XLA Modules:
  0.0 89.2 jit_solution(13185221816535631621)
XLA Ops:
  0.6 2.2 %prepare.1 = (bf16[128,1024]{1,0:T(8,128)(2,1)}, bf16[128,1024]{1,0:T(8,128)(2,1)}) custom-call(bf16[128,1024]{1,0:T(8,128)(2,1)} %bitcast.8, bf16[128,1024]{1,0:T(8,128)(2,1)} %bitcast.12, bf16[128,1024]{1,0:T(8,128)(2,1)} %bitcast.10), custom_call_target="tpu_custom_call" | custom-call | flops 40000000 | bytes 1400000 | tf_op jit(solution)/shard_map/prepare/pallas_call | solution.py:35
  2.8 3.8 %collective-permute-start = (bf16[128,1024]{1,0:T(8,128)(2,1)}, bf16[128,1024]{1,0:T(8,128)(2,1)S(1)}, u32[]{:S(2)}, u32[]{:S(2)}) collective-permute-start(bf16[128,1024]{1,0:T(8,128)(2,1)} %get-tuple-element.12.refs_1_.refs_2_.refs_4_), channel_id=1, source_target_pairs={{0,8},{4,12},{8,16},{12,20},{16,24},{20,28},{24,32},{28,36},{32,40... | collective-permute-start | bytes 786440 | tf_op jit(solution)/shard_map/ppermute | solution.py:281
  6.6 0.0 copy-start
  6.6 0.0 copy-start.1
  6.6 1.4 %collective-permute-start.2 = (bf16[128,1024]{1,0:T(8,128)(2,1)}, bf16[128,1024]{1,0:T(8,128)(2,1)S(1)}, u32[]{:S(2)}, u32[]{:S(2)}) collective-permute-start(bf16[128,1024]{1,0:T(8,128)(2,1)} %get-tuple-element.13.refs_4_.refs_6_.refs_1_), channel_id=1, source_target_pairs={{8,0},{12,4},{16,8},{20,12},{24,16},{28,20},{32,24},{36,28},{40,32... | collective-permute-start | bytes 786440 | tf_op jit(solution)/shard_map/ppermute | solution.py:281
  8.1 1.9 %collective-permute-start.7 = (bf16[128,1024]{1,0:T(8,128)(2,1)}, bf16[128,1024]{1,0:T(8,128)(2,1)S(1)}, u32[]{:S(2)}, u32[]{:S(2)}) collective-permute-start(bf16[128,1024]{1,0:T(8,128)(2,1)} %get-tuple-element.13.refs_4_.refs_6_.refs_1_), channel_id=1, source_target_pairs={{0,4},{4,0},{8,12},{12,8},{16,20},{20,16},{24,28},{28,24},{32,36},... | collective-permute-start | bytes 786440 | tf_op jit(solution)/shard_map/ppermute | solution.py:285
  10.0 2.5 %collective-permute-done.refs_2_.refs_3_.refs_5_ = bf16[128,1024]{1,0:T(8,128)(2,1)S(1)} collective-permute-done((bf16[128,1024]{1,0:T(8,128)(2,1)}, bf16[128,1024]{1,0:T(8,128)(2,1)S(1)}, u32[]{:S(2)}, u32[]{:S(2)}) %collective-permute-start) | collective-permute-done | bytes 262176 | tf_op jit(solution)/shard_map/ppermute | solution.py:281
  12.5 4.3 %collective-permute-start.1 = (bf16[128,1024]{1,0:T(8,128)(2,1)S(1)}, bf16[128,1024]{1,0:T(8,128)(2,1)S(1)}, u32[]{:S(2)}, u32[]{:S(2)}) collective-permute-start(bf16[128,1024]{1,0:T(8,128)(2,1)S(1)} %collective-permute-done.refs_2_.refs_3_.refs_5_), channel_id=1, source_target_pairs={{0,8},{4,12},{8,16},{12,20},{16,24},{20,28},{24,32},{28,36},{32,40... | collective-permute-start | bytes 786440 | tf_op jit(solution)/shard_map/ppermute | solution.py:281
  16.8 0.1 collective-permute-done.2.refs_5_.refs_7_.refs_3_
  16.8 1.3 %collective-permute-start.3 = (bf16[128,1024]{1,0:T(8,128)(2,1)S(1)}, bf16[128,1024]{1,0:T(8,128)(2,1)S(1)}, u32[]{:S(2)}, u32[]{:S(2)}) collective-permute-start(bf16[128,1024]{1,0:T(8,128)(2,1)S(1)} %collective-permute-done.2.refs_5_.refs_7_.refs_3_), channel_id=1, source_target_pairs={{8,0},{12,4},{16,8},{20,12},{24,16},{28,20},{32,24},{36,28},{40,32... | collective-permute-start | bytes 786440 | tf_op jit(solution)/shard_map/ppermute | solution.py:281
  18.1 4.7 %toeplitz.1 = (bf16[32,128,384]{2,1,0:T(8,128)(2,1)}, bf16[32,128,384]{2,1,0:T(8,128)(2,1)}) custom-call(bf16[32,640]{1,0:T(8,128)(2,1)} %taps_ref.1), custom_call_target="tpu_custom_call" | custom-call | flops 8000000000 | bytes 6400000 | tf_op jit(solution)/shard_map/toeplitz/pallas_call | solution.py:63
  22.8 0.0 collective-permute-done.1.refs_3_.refs_4_
  22.8 0.7 collective-permute-start.4
  23.5 2.5 %collective-permute-done.3.refs_6_.refs_8_ = bf16[128,1024]{1,0:T(8,128)(2,1)S(1)} collective-permute-done((bf16[128,1024]{1,0:T(8,128)(2,1)S(1)}, bf16[128,1024]{1,0:T(8,128)(2,1)S(1)}, u32[]{:S(2)}, u32[]{:S(2)}) %collective-permute-start.3) | collective-permute-done | bytes 262176 | tf_op jit(solution)/shard_map/ppermute | solution.py:281
  26.0 1.3 %collective-permute-start.5 = (bf16[128,1024]{1,0:T(8,128)(2,1)S(1)}, bf16[128,1024]{1,0:T(8,128)(2,1)S(1)}, u32[]{:S(2)}, u32[]{:S(2)}) collective-permute-start(bf16[128,1024]{1,0:T(8,128)(2,1)S(1)} %collective-permute-done.3.refs_6_.refs_8_), channel_id=1, source_target_pairs={{8,0},{16,8},{24,16},{32,24},{40,32},{48,40},{56,48},{64,56},{72,6... | collective-permute-start | bytes 786440 | tf_op jit(solution)/shard_map/ppermute | solution.py:281
  27.3 0.0 collective-permute-done.7.refs_2_
  27.3 4.8 %pair_near.1.refs_1_ = f32[8,4,640]{2,1,0:T(4,128)S(1)} custom-call(s32[1]{0:T(128)} %bitcast.3.refs_0_, bf16[128,1024]{1,0:T(8,128)(2,1)S(1)} %copy-done, bf16[128,1024]{1,0:T(8,128)(2,1)S(1)} %collective-permute-done.7.refs_2_, bf16[128,1024]{1,0:T(8,128)(2,1)S(1)} %collective-permute-done.2.refs_5_.refs_7_.refs_3_, bf16[128,1024]{1,0:T(8,128)(2,1)S(1)} %copy-done.1, ...), custom_call_target="tpu_custom_call" | custom-call | flops 8000000000 | bytes 1500000 | tf_op jit(solution)/shard_map/pair_near/pallas_call | solution.py:173
  32.1 0.0 collective-permute-done.4.refs_5_
  32.1 3.4 %collective-permute-done.5.refs_9_ = bf16[128,1024]{1,0:T(8,128)(2,1)S(1)} collective-permute-done((bf16[128,1024]{1,0:T(8,128)(2,1)S(1)}, bf16[128,1024]{1,0:T(8,128)(2,1)S(1)}, u32[]{:S(2)}, u32[]{:S(2)}) %collective-permute-start.5) | collective-permute-done | bytes 262176 | tf_op jit(solution)/shard_map/ppermute | solution.py:281
  35.5 0.0 copy-done.5
  35.5 3.3 %convolve_cross.1 = f32[2,128,1024]{2,1,0:T(8,128)S(1)} custom-call(s32[1]{0:T(128)} %bitcast.3.refs_0_, bf16[32,128,384]{2,1,0:T(8,128)(2,1)S(1)} %copy-done.6, bf16[128,1024]{1,0:T(8,128)(2,1)S(1)} %copy-done.1, bf16[128,1024]{1,0:T(8,128)(2,1)S(1)} %collective-permute-done.refs_2_.refs_3_.refs_5_, ...), custom_call_target="tpu_custom_call" | custom-call | flops 5000000000 | bytes 5500000 | tf_op jit(solution)/shard_map/convolve_cross/pallas_call | solution.py:247
  38.8 1.9 %collective-permute-start.6 = (f32[2,128,1024]{2,1,0:T(8,128)S(1)}, f32[2,128,1024]{2,1,0:T(8,128)}, u32[]{:S(2)}, u32[]{:S(2)}) collective-permute-start(f32[2,128,1024]{2,1,0:T(8,128)S(1)} %convolve_cross.1), channel_id=1, source_target_pairs={{0,4},{4,0},{8,12},{12,8},{16,20},{20,16},{24,28},{28,24},{32,36},... | collective-permute-start | bytes 3145736 | tf_op jit(solution)/shard_map/ppermute | solution.py:285
  40.7 0.0 copy-done.2
  40.7 0.0 copy-done.4
  40.7 4.6 %pair_far.1 = f32[128,1,160]{2,1,0:T(1,128)} custom-call(s32[1]{0:T(128)} %bitcast.3.refs_0_, f32[8,4,640]{2,1,0:T(4,128)S(1)} %pair_near.1.refs_1_, bf16[128,1024]{1,0:T(8,128)(2,1)S(1)} %collective-permute-done.7.refs_2_, bf16[128,1024]{1,0:T(8,128)(2,1)S(1)} %collective-permute-done.refs_2_.refs_3_.refs_5_, ...), custom_call_target="tpu_custom_call" | custom-call | flops 4000000000 | bytes 1500000 | tf_op jit(solution)/shard_map/pair_far/pallas_call | solution.py:183
  45.3 20.6 %all-to-all-start = ((f32[128,1,160]{2,1,0:T(1,128)}), f32[128,1,160]{2,1,0:T(1,128)S(1)}, u32[]{:S(2)}, u32[]{:S(2)}) async-start(f32[128,1,160]{2,1,0:T(1,128)} %pair_far.1), calls=%async_computation | async-start | bytes 262144 | tf_op jit(solution)/shard_map/all_to_all | solution.py:313
  65.9 7.0 %convolve_own.1.own_ref = f32[2,128,1024]{2,1,0:T(8,128)} custom-call(bf16[32,128,384]{2,1,0:T(8,128)(2,1)} %get-tuple-element.11.refs_0_, bf16[128,1024]{1,0:T(8,128)(2,1)} %get-tuple-element.12.refs_1_.refs_2_.refs_4_, bf16[128,1024]{1,0:T(8,128)(2,1)} %copy-done.2, bf16[128,1024]{1,0:T(8,128)(2,1)} %copy-done.4, ...), custom_call_target="tpu_custom_call" | custom-call | flops 5000000000 | bytes 5500000 | tf_op jit(solution)/shard_map/convolve_own/pallas_call | solution.py:247
  72.9 11.2 %all-to-all-done = f32[128,1,160]{2,1,0:T(1,128)S(1)} async-done(((f32[128,1,160]{2,1,0:T(1,128)}), f32[128,1,160]{2,1,0:T(1,128)S(1)}, u32[]{:S(2)}, u32[]{:S(2)}) %all-to-all-start) | async-done | bytes 81952 | tf_op jit(solution)/shard_map/all_to_all | solution.py:313
  84.1 0.2 reduce_sum.9
  84.3 0.7 div.12
  85.0 0.0 collective-permute-done.6.met_ref
  85.0 4.3 %finish.1 = (bf16[128,1024]{1,0:T(8,128)(2,1)}, bf16[128,1024]{1,0:T(8,128)(2,1)}, bf16[128,1024]{1,0:T(8,128)(2,1)}) custom-call(bf16[128,1024]{1,0:T(8,128)(2,1)} %bitcast.9, bf16[128,1024]{1,0:T(8,128)(2,1)} %bitcast.11, f32[2,128,1024]{2,1,0:T(8,128)} %convolve_own.1.own_ref, f32[2,128,1024]{2,1,0:T(8,128)} %collective-permute-done.6.met_ref), custom_call_target="tpu_custom_call" | custom-call | flops 200000000 | bytes 3500000 | tf_op jit(solution)/shard_map/finish/pallas_call | solution.py:267
  (10 shorter events, 0.0 us)
Async XLA Ops:
  2.8 9.7 %collective-permute-start = (bf16[128,1024]{1,0:T(8,128)(2,1)}, bf16[128,1024]{1,0:T(8,128)(2,1)S(1)}, u32[]{:S(2)}, u32[]{:S(2)}) collective-permute-start(bf16[128,1024]{1,0:T(8,128)(2,1)} %get-tuple-element.12.refs_1_.refs_2_.refs_4_), channel_id=1, source_target_pairs={{0,8},{4,12},{8,16},{12,20},{16,24},{20,28},{24,32},{28,36},{32,40... | collective-permute-start | bytes 786440 | tf_op jit(solution)/shard_map/ppermute | solution.py:281
  6.6 20.7 %copy-start = (bf16[128,1024]{1,0:T(8,128)(2,1)S(1)}, bf16[128,1024]{1,0:T(8,128)(2,1)}, u32[]{:S(2)}) copy-start(bf16[128,1024]{1,0:T(8,128)(2,1)} %get-tuple-element.13.refs_4_.refs_6_.refs_1_) | copy-start | bytes 786436
  6.6 20.7 %copy-start.1 = (bf16[128,1024]{1,0:T(8,128)(2,1)S(1)}, bf16[128,1024]{1,0:T(8,128)(2,1)}, u32[]{:S(2)}) copy-start(bf16[128,1024]{1,0:T(8,128)(2,1)} %get-tuple-element.12.refs_1_.refs_2_.refs_4_) | copy-start | bytes 786436
  6.6 10.2 %collective-permute-start.2 = (bf16[128,1024]{1,0:T(8,128)(2,1)}, bf16[128,1024]{1,0:T(8,128)(2,1)S(1)}, u32[]{:S(2)}, u32[]{:S(2)}) collective-permute-start(bf16[128,1024]{1,0:T(8,128)(2,1)} %get-tuple-element.13.refs_4_.refs_6_.refs_1_), channel_id=1, source_target_pairs={{8,0},{12,4},{16,8},{20,12},{24,16},{28,20},{32,24},{36,28},{40,32... | collective-permute-start | bytes 786440 | tf_op jit(solution)/shard_map/ppermute | solution.py:281
  8.1 19.2 %collective-permute-start.7 = (bf16[128,1024]{1,0:T(8,128)(2,1)}, bf16[128,1024]{1,0:T(8,128)(2,1)S(1)}, u32[]{:S(2)}, u32[]{:S(2)}) collective-permute-start(bf16[128,1024]{1,0:T(8,128)(2,1)} %get-tuple-element.13.refs_4_.refs_6_.refs_1_), channel_id=1, source_target_pairs={{0,4},{4,0},{8,12},{12,8},{16,20},{20,16},{24,28},{28,24},{32,36},... | collective-permute-start | bytes 786440 | tf_op jit(solution)/shard_map/ppermute | solution.py:285
  12.5 28.2 %copy-start.2 = (bf16[128,1024]{1,0:T(8,128)(2,1)}, bf16[128,1024]{1,0:T(8,128)(2,1)S(1)}, u32[]{:S(2)}) copy-start(bf16[128,1024]{1,0:T(8,128)(2,1)S(1)} %collective-permute-done.refs_2_.refs_3_.refs_5_) | copy-start | bytes 786436
  12.5 10.3 %collective-permute-start.1 = (bf16[128,1024]{1,0:T(8,128)(2,1)S(1)}, bf16[128,1024]{1,0:T(8,128)(2,1)S(1)}, u32[]{:S(2)}, u32[]{:S(2)}) collective-permute-start(bf16[128,1024]{1,0:T(8,128)(2,1)S(1)} %collective-permute-done.refs_2_.refs_3_.refs_5_), channel_id=1, source_target_pairs={{0,8},{4,12},{8,16},{12,20},{16,24},{20,28},{24,32},{28,36},{32,40... | collective-permute-start | bytes 786440 | tf_op jit(solution)/shard_map/ppermute | solution.py:281
  16.8 18.6 %copy-start.3 = (bf16[128,1024]{1,0:T(8,128)(2,1)}, bf16[128,1024]{1,0:T(8,128)(2,1)S(1)}, u32[]{:S(2)}) copy-start(bf16[128,1024]{1,0:T(8,128)(2,1)S(1)} %collective-permute-done.2.refs_5_.refs_7_.refs_3_) | copy-start | bytes 786436
  16.8 9.2 %collective-permute-start.3 = (bf16[128,1024]{1,0:T(8,128)(2,1)S(1)}, bf16[128,1024]{1,0:T(8,128)(2,1)S(1)}, u32[]{:S(2)}, u32[]{:S(2)}) collective-permute-start(bf16[128,1024]{1,0:T(8,128)(2,1)S(1)} %collective-permute-done.2.refs_5_.refs_7_.refs_3_), channel_id=1, source_target_pairs={{8,0},{12,4},{16,8},{20,12},{24,16},{28,20},{32,24},{36,28},{40,32... | collective-permute-start | bytes 786440 | tf_op jit(solution)/shard_map/ppermute | solution.py:281
  22.8 17.9 %copy-start.4 = (bf16[128,1024]{1,0:T(8,128)(2,1)}, bf16[128,1024]{1,0:T(8,128)(2,1)S(1)}, u32[]{:S(2)}) copy-start(bf16[128,1024]{1,0:T(8,128)(2,1)S(1)} %collective-permute-done.1.refs_3_.refs_4_) | copy-start | bytes 786436
  22.8 9.3 %collective-permute-start.4 = (bf16[128,1024]{1,0:T(8,128)(2,1)S(1)}, bf16[128,1024]{1,0:T(8,128)(2,1)S(1)}, u32[]{:S(2)}, u32[]{:S(2)}) collective-permute-start(bf16[128,1024]{1,0:T(8,128)(2,1)S(1)} %collective-permute-done.1.refs_3_.refs_4_), channel_id=1, source_target_pairs={{4,12},{12,20},{20,28},{28,36},{36,44},{44,52},{52,60},{60,68},{68... | collective-permute-start | bytes 786440 | tf_op jit(solution)/shard_map/ppermute | solution.py:281
  26.0 9.5 %copy-start.5 = (bf16[128,1024]{1,0:T(8,128)(2,1)}, bf16[128,1024]{1,0:T(8,128)(2,1)S(1)}, u32[]{:S(2)}) copy-start(bf16[128,1024]{1,0:T(8,128)(2,1)S(1)} %collective-permute-done.3.refs_6_.refs_8_) | copy-start | bytes 786436
  26.0 9.5 %collective-permute-start.5 = (bf16[128,1024]{1,0:T(8,128)(2,1)S(1)}, bf16[128,1024]{1,0:T(8,128)(2,1)S(1)}, u32[]{:S(2)}, u32[]{:S(2)}) collective-permute-start(bf16[128,1024]{1,0:T(8,128)(2,1)S(1)} %collective-permute-done.3.refs_6_.refs_8_), channel_id=1, source_target_pairs={{8,0},{16,8},{24,16},{32,24},{40,32},{48,40},{56,48},{64,56},{72,6... | collective-permute-start | bytes 786440 | tf_op jit(solution)/shard_map/ppermute | solution.py:281
  27.3 8.2 %copy-start.6 = (bf16[32,128,384]{2,1,0:T(8,128)(2,1)S(1)}, bf16[32,128,384]{2,1,0:T(8,128)(2,1)}, u32[]{:S(2)}) copy-start(bf16[32,128,384]{2,1,0:T(8,128)(2,1)} %get-tuple-element.14.refs_1_) | copy-start | bytes 9437188
  38.8 46.2 %collective-permute-start.6 = (f32[2,128,1024]{2,1,0:T(8,128)S(1)}, f32[2,128,1024]{2,1,0:T(8,128)}, u32[]{:S(2)}, u32[]{:S(2)}) collective-permute-start(f32[2,128,1024]{2,1,0:T(8,128)S(1)} %convolve_cross.1), channel_id=1, source_target_pairs={{0,4},{4,0},{8,12},{12,8},{16,20},{20,16},{24,28},{28,24},{32,36},... | collective-permute-start | bytes 3145736 | tf_op jit(solution)/shard_map/ppermute | solution.py:285
  45.3 38.8 %all-to-all-start = ((f32[128,1,160]{2,1,0:T(1,128)}), f32[128,1,160]{2,1,0:T(1,128)S(1)}, u32[]{:S(2)}, u32[]{:S(2)}) async-start(f32[128,1,160]{2,1,0:T(1,128)} %pair_far.1), calls=%async_computation | async-start | bytes 262144 | tf_op jit(solution)/shard_map/all_to_all | solution.py:313
